TPU v7x, 1024 devices: a whole 8x8x8 slice. The times are simulated.
1024 devices in a mesh: band: 32 (over z_lo, y, core), col: 32 (over z_hi, x).
Axes of the slice: x: 8, y: 8, z: 8 (z_hi: 4, z_lo: 2; z = z_hi * 2 + z_lo), core: 2. Of those that a mesh axis runs over, the one named last changes fastest.
Arguments:
- intersections: bfloat16 [64, 4096, 512], P('band'), may hold values from -6 to 6
- screened: bfloat16 [4096, 4096], P('band', 'col'), may hold values from -0.09375 to 0.09375
- poles: bfloat16 [4096, 4096], P('band', 'col'), may hold values from 0.5 to 4
- gap_energy: float32 [3], replicated, may hold values from 0.3 to 3
- gap_class: int32 [64, 512], P('band'), may hold values from 0 to 2
Outputs:
- sigma: float32 [512, 512], P('band', 'col')
All inputs are finite; a program needn't handle non-finite values.
Results may differ from a plain program's by a relative error of at most 0.0041.
Values may be sent and summed in bfloat16 or wider, within the bound.
No kernel may reach another device: no remote copies, remote signals or barrier semaphores. Data moves between devices by JAX's collectives and lax.ppermute only.
A program may use at most 64 MiB of HBM per device.

v0:
```python
import jax
import jax.numpy as jnp
from jax import lax
from jax.sharding import PartitionSpec as P


def make_factors(amp_piece, pole_piece, gap_energy, classes):
    amps = amp_piece.astype(jnp.float32)
    freqs = pole_piece.astype(jnp.float32)
    result = []
    for class_id in range(classes):
        energy = gap_energy[class_id]
        result.append((amps * freqs / (freqs * freqs + energy * energy)).astype(jnp.bfloat16))
    return result


def local(intersections, screened, poles, gap_energy, gap_class):
    bands = intersections.shape[0]
    states = intersections.shape[2]
    columns = screened.shape[1]
    classes = gap_energy.shape[0]
    col_pos = lax.axis_index("col")
    amp_piece = lax.all_gather(screened, "band", axis=0, tiled=True)
    pole_piece = lax.all_gather(poles, "band", axis=0, tiled=True)
    factors = make_factors(amp_piece, pole_piece, gap_energy, classes)
    updated = []
    for add_band_idx in range(bands):
        for add_class_id in range(classes):
            term = lax.dot_general(
                intersections[add_band_idx],
                factors[add_class_id],
                (((0,), (0,)), ((), ())),
                preferred_element_type=jnp.float32,
            )
            updated.append(term)
    sides = tuple(updated)
    partial_value = jnp.zeros((states, states), jnp.float32)
    for band_idx in range(bands):
        side = jnp.zeros((states, columns), jnp.float32)
        for class_id in range(classes):
            picked = (gap_class[band_idx] == class_id).astype(jnp.float32)
            side = side + picked[:, None] * sides[band_idx * classes + class_id]
        right = lax.dynamic_slice_in_dim(intersections[band_idx], col_pos * columns, columns, 0)
        partial_value = partial_value + jnp.dot(
            side.astype(jnp.bfloat16), right, preferred_element_type=jnp.float32
        )
    total_g = columns * lax.axis_size("col")
    total_bands = bands * lax.axis_size("band")
    scale = 1.0 / jnp.sqrt(jnp.float32(total_g * total_bands))
    row_count = states // lax.axis_size("band")
    col_count = states // lax.axis_size("col")
    summed = lax.psum(partial_value, ("band", "col"))
    rows_part = lax.dynamic_slice_in_dim(summed, lax.axis_index("band") * row_count, row_count, 0)
    block = lax.dynamic_slice_in_dim(rows_part, col_pos * col_count, col_count, 1)
    return block * scale


def solution(mesh):
    return jax.shard_map(
        local,
        mesh=mesh,
        in_specs=(P("band", None, None), P("band", "col"), P("band", "col"), P(), P("band", None)),
        out_specs=P("band", "col"),
        check_vma=False,
    )
```

profile of v0, /device:TPU:1, one launch (start us, length us, event | category | flops | bytes accessed | tf_op | source)
XLA Modules:
  0.0 483.1 jit_solution(10204704046218690629)
XLA Ops:
  6.5 0.0 all-gather.3.cloned.1.call-start
  6.5 0.7 all-gather.3.cloned.1.call-update
  7.3 0.0 all-gather.5.cloned.1.call-start
  7.3 0.7 all-gather.5.cloned.1.call-update
  8.0 0.0 all-reduce.2.cloned.1.call-start
  8.1 1.4 fusion.83
  13.1 0.8 compare_convert_fusion.2
  13.9 5.7 %fusion.82 = (bf16[1,4096,512]{2,1,0:T(8,128)(2,1)}, bf16[1,4096,512]{2,1,0:T(8,128)(2,1)}) fusion(bf16[2,4096,512]{2,1,0:T(8,128)(2,1)} %param.5), kind=kLoop, calls=%fused_computation.56 | loop fusion | bytes 16777216 | tf_op jit(solution)/shard_map/slice | solution.py:30
  19.6 72.1 %all-gather.3.cloned.1.call-done = bf16[4096,128]{1,0:T(8,128)(2,1)} async-done(((bf16[128,128]{1,0:T(8,128)(2,1)}), bf16[4096,128]{1,0:T(8,128)(2,1)}) %all-gather.3.cloned.1.call-update) | async-done | bytes 1048592 | tf_op jit(solution)/shard_map/all_gather | solution.py:23
  91.8 72.0 %all-gather.5.cloned.1.call-done = bf16[4096,128]{1,0:T(8,128)(2,1)} async-done(((bf16[128,128]{1,0:T(8,128)(2,1)}), bf16[4096,128]{1,0:T(8,128)(2,1)}) %all-gather.5.cloned.1.call-update) | async-done | bytes 1048592 | tf_op jit(solution)/shard_map/all_gather | solution.py:24
  163.8 0.0 copy-start
  163.8 0.0 copy-start.1
  163.8 4.5 fusion.30
  168.3 0.8 copy-done
  169.1 0.2 copy-done.1
  169.3 0.3 copy-done.2
  169.6 0.8 fusion.45
  170.4 1.6 fusion.33
  172.0 1.5 fusion.48
  173.6 3.4 fusion.58
  177.0 4.4 convolution_add_fusion
  181.4 0.0 all-reduce.2.cloned.1.call-update
  181.4 293.8 %all-reduce.2.cloned.1.call-done = f32[512,512]{1,0:T(8,128)} async-done(((f32[512,512]{1,0:T(8,128)}), f32[512,512]{1,0:T(8,128)}) %all-reduce.2.cloned.1.call-update) | async-done | bytes 1048592 | tf_op jit(solution)/shard_map/psum | solution.py:52
  475.2 1.4 dynamic-slice_multiply_fusion
  (1 shorter events, 0.0 us)
Async XLA Ops:
  6.5 85.2 %all-gather.3.cloned.1.call-start = ((), (), s32[]{:S(2)}) async-start(), calls=%async_computation | async-start | bytes 1081344 | tf_op jit(solution)/shard_map/all_gather | solution.py:23
  7.3 156.5 %all-gather.5.cloned.1.call-start = ((), (), s32[]{:S(2)}) async-start(), calls=%async_computation.1 | async-start | bytes 1081344 | tf_op jit(solution)/shard_map/all_gather | solution.py:24
  8.0 467.2 %all-reduce.2.cloned.1.call-start = ((), (), s32[]{:S(2)}) async-start(), calls=%async_computation.2 | async-start | bytes 2097152 | tf_op jit(solution)/shard_map/psum | solution.py:52
  163.8 5.3 %copy-start = (bf16[2,4096,512]{2,1,0:T(8,128)(2,1)S(1)}, bf16[2,4096,512]{2,1,0:T(8,128)(2,1)}, u32[]{:S(2)}) copy-start(bf16[2,4096,512]{2,1,0:T(8,128)(2,1)} %param.5) | copy-start | bytes 25165828
  163.8 5.5 %copy-start.1 = (bf16[4096,128]{1,0:T(8,128)(2,1)S(1)}, bf16[4096,128]{1,0:T(8,128)(2,1)}, u32[]{:S(2)}) copy-start(bf16[4096,128]{1,0:T(8,128)(2,1)} %all-gather.3.cloned.1.call-done) | copy-start | bytes 3145732
  163.8 5.8 %copy-start.2 = (bf16[4096,128]{1,0:T(8,128)(2,1)S(1)}, bf16[4096,128]{1,0:T(8,128)(2,1)}, u32[]{:S(2)}) copy-start(bf16[4096,128]{1,0:T(8,128)(2,1)} %all-gather.5.cloned.1.call-done) | copy-start | bytes 3145732
Sparse Core Ops, SparseCore 0:
  10.1 81.6 all-gather.2
  94.5 69.2 all-gather.4
  181.5 293.6 all-reduce.1
where the time goes:
time: 483 us
  waiting for transfers between devices  439 us (91%)
  between operations  16.8 us (3%)
  matrix products  16.2 us (3%)
  local copies, waits for them, and re-layouts  8.44 us (2%)
    psum x1, waiting for transfers between devices, local(): summed = lax.psum(partial_value, ('band', 'col'))  294 us
    all_gather x1, waiting for transfers between devices, local(): amp_piece = lax.all_gather(screened, 'band', axis=0, tiled=True)  72.1 us
    all_gather x1, waiting for transfers between devices, local(): pole_piece = lax.all_gather(poles, 'band', axis=0, tiled=True)  72 us
  transfers between devices with their start and end apart: 3, of which 3 were waited for; matrix products, arithmetic and copies ran while one was open for 2% of the time, Pallas kernels for 0%

commit v1 on v0

v1 whole, which is shorter than its diff:
```python
import jax
import jax.numpy as jnp
from jax import lax
from jax.experimental import pallas as pl
from jax.experimental.pallas import tpu as pltpu
from jax.sharding import Mesh, PartitionSpec as P

CLASSES = 3
F32 = jnp.float32
BF16 = jnp.bfloat16


def body(place, energy, y_ref, z_ref, cy_ref, cz_ref, inter_ref, right_ref, class_ref, keep_ref, send_ref, side_acc, full):
    step = pl.program_id(0)
    bands, blocks, size, states = inter_ref.shape
    squares = [energy[c] * energy[c] for c in range(CLASSES)]

    @pl.when(step == 0)
    def _():
        side_acc[...] = jnp.zeros_like(side_acc)

    def add(group):
        half = lax.rem(step, 2) * blocks
        columns = [[] for _ in range(CLASSES)]
        for j in range(blocks):
            amps = group[half + j, 0].astype(F32)
            freqs = group[half + j, 1].astype(F32)
            square = freqs * freqs
            d0, d1, d2 = (square + e for e in squares)
            d12 = d1 * d2
            ratio = amps * freqs / (d0 * d12)
            r0 = ratio * d0
            columns[0].append((ratio * d12).astype(BF16))
            columns[1].append((r0 * d2).astype(BF16))
            columns[2].append((r0 * d1).astype(BF16))
        factor = jnp.concatenate([jnp.concatenate(c, axis=1) for c in columns], axis=0)
        for b in range(bands):
            rows = inter_ref[b].reshape(blocks * size, states)
            side_acc[b] += jnp.dot(factor, rows, preferred_element_type=F32)

    for k, group in enumerate((y_ref, cy_ref, z_ref, cz_ref)):
        pl.when(step // 2 == k)(lambda group=group: add(group))

    @pl.when(step == pl.num_programs(0) - 1)
    def _():
        sides = []
        for b in range(bands):
            kind = class_ref[b : b + 1, :]
            side = jnp.zeros((size, states), F32)
            for c in range(CLASSES):
                side = jnp.where(kind == c, side_acc[b, c * size : (c + 1) * size, :], side)
            sides.append(side.astype(BF16))
        left = jnp.concatenate(sides, axis=0)
        right = right_ref[...].reshape(bands * size, states)
        total = lax.dot_general(left, right, (((0,), (0,)), ((), ())), preferred_element_type=F32)
        full[...] = total.reshape(full.shape)
        core = place[1]
        keep_ref[...] = full[:, core]
        send_ref[...] = full[:, 1 - core]


def terms(place, gap_energy, groups, intersections, gap_class):
    bands, rows, states = intersections.shape
    size = groups[0].shape[-1]
    per = rows // (2 * 2 * size)
    blocks = per // 2
    split = intersections.reshape(bands, 2, per, 2, size, states)
    flat = intersections.reshape(bands, rows // size, size, states)

    def rows_of(t, place):
        k = t // 2
        return (0, (place[0] + k // 2) % 2, t % 2, (place[1] + k % 2) % 2, 0, 0)

    whole = pl.BlockSpec(groups[0].shape, lambda t, place: (0, 0, 0, 0))
    fine = 16
    outer = states // (2 * fine)
    half = jax.ShapeDtypeStruct((outer, fine, states), F32)
    return pl.pallas_call(
        body,
        out_shape=(half, half),
        grid_spec=pltpu.PrefetchScalarGridSpec(
            num_scalar_prefetch=1,
            grid=(8,),
            in_specs=[
                pl.BlockSpec(memory_space=pltpu.SMEM),
                whole,
                whole,
                whole,
                whole,
                pl.BlockSpec((bands, None, blocks, None, size, states), rows_of),
                pl.BlockSpec((bands, None, size, states), lambda t, place: (0, place[2], 0, 0)),
                pl.BlockSpec(gap_class.shape, lambda t, place: (0, 0)),
            ],
            out_specs=[pl.BlockSpec(half.shape, lambda t, place: (0, 0, 0))] * 2,
            scratch_shapes=[
                pltpu.VMEM((bands, CLASSES * size, states), F32),
                pltpu.VMEM((outer, 2, fine, states), F32),
            ],
        ),
        compiler_params=pltpu.CompilerParams(dimension_semantics=("arbitrary",), vmem_limit_bytes=50 << 20),
        cost_estimate=pl.CostEstimate(flops=3 << 30, bytes_accessed=12 << 20, transcendentals=0),
        name="terms",
    )(place, gap_energy, *groups, split, flat, gap_class)


def local(intersections, screened, poles, gap_energy, gap_class):
    zl, y, c = lax.axis_index("zl"), lax.axis_index("y"), lax.axis_index("c")
    column = lax.axis_index("zh") * lax.axis_size("x") + lax.axis_index("x")
    place = jnp.stack([zl, c, column]).astype(jnp.int32)
    swap = [(0, 1), (1, 0)]
    own = jnp.stack([screened.T, poles.T])
    per = lax.axis_size("y")
    y_group = lax.all_to_all(jnp.broadcast_to(own[None], (per,) + own.shape), "y", 0, 0, tiled=True)
    z_group = lax.ppermute(y_group, "zl", swap)
    cy_group = lax.ppermute(y_group, "c", swap)
    cz_group = lax.ppermute(z_group, "c", swap)
    keep, send = terms(place, gap_energy, (y_group, z_group, cy_group, cz_group), intersections, gap_class)
    chip = keep + lax.ppermute(send, "c", swap)
    pieces = lax.all_to_all(chip.astype(BF16), ("zl", "y"), 0, 0, tiled=True)
    rows = jnp.sum(pieces.astype(F32), axis=0)
    columns = lax.axis_size("zh") * lax.axis_size("x")
    fine = rows.shape[0]
    split = rows.reshape(fine, columns, -1).transpose(1, 0, 2)
    wide = split.shape[2]
    blocks = lax.all_to_all(split.reshape(columns, fine * wide), ("zh", "x"), 0, 0, tiled=True)
    total = jnp.sum(blocks, axis=0).reshape(fine, wide)
    count = intersections.shape[1] * intersections.shape[0] * 2 * per * 2
    return total * (1.0 / jnp.sqrt(F32(count)))


def solution(mesh):
    fine = Mesh(mesh.devices.reshape(2, 8, 2, 4, 8), ("zl", "y", "c", "zh", "x"))
    band, col = ("zl", "y", "c"), ("zh", "x")
    return jax.shard_map(
        local,
        mesh=fine,
        in_specs=(P(band, None, None), P(band, col), P(band, col), P(), P(band, None)),
        out_specs=P(band, col),
        check_vma=False,
    )
```

time: 483 us -> 109 us (0.23)
  the two profiles are of different devices: /device:TPU:1 before, /device:TPU:16 now
where the time goes in v1:
time: 109 us; the launch traced here: 108 us
  blocking collectives  76 us (70%)
  waiting for transfers between devices  11 us (10%)
  Pallas kernels  9.88 us (9%)
  starting transfers between devices  7.78 us (7%)
  local copies, waits for them, and re-layouts  2.56 us (2%)
    all_to_all x1, blocking collectives, local(): lax.all_to_all(split.reshape(columns, fine * wide), ('zh', 'x'), 0, 0, ti...  32.4 us
    all_to_all x1, blocking collectives, local(): lax.all_to_all(jnp.broadcast_to(own[None], (per,) + own.shape), 'y', 0, 0...  27.2 us
    all_to_all x1, blocking collectives, local(): pieces = lax.all_to_all(chip.astype(BF16), ('zl', 'y'), 0, 0, tiled=True)  16.3 us
    pallas_call x1, Pallas kernels, terms(): pl.pallas_call(body, out_shape=(half, half), grid_spec=pltpu.PrefetchScal...  9.88 us
    ppermute x1, waiting for transfers between devices, local(): z_group = lax.ppermute(y_group, 'zl', swap)  7.44 us
  transfers between devices with their start and end apart: 4, of which 3 were waited for; matrix products, arithmetic and copies ran while one was open for 0% of the time, Pallas kernels for 0%

profile of v1, /device:TPU:16, one launch (start us, length us, event | category | flops | bytes accessed | tf_op | source)
XLA Modules:
  0.0 108.3 jit_solution(610950591436022872)
XLA Ops:
  0.0 0.8 pad_maximum_fusion
  0.8 0.1 copy.9
  0.9 0.1 broadcast_in_dim.2
  1.0 27.2 %all_to_all.19.y_ref = bf16[8,2,128,128]{3,2,1,0:T(8,128)(2,1)S(1)} all-to-all(bf16[8,2,128,128]{3,2,1,0:T(8,128)(2,1)S(1)} %broadcast_in_dim.2), channel_id=1, replica_groups=mesh['zl'=2,'y'=8,'c'=2,'zh'=4,'x'=8] {'y'}, dimensions={0} | all-to-all | bytes 1048576 | tf_op jit(solution)/shard_map/all_to_all | solution.py:113
  28.2 1.9 %collective-permute-start = (bf16[8,2,128,128]{3,2,1,0:T(8,128)(2,1)S(1)}, bf16[8,2,128,128]{3,2,1,0:T(8,128)(2,1)S(1)}, u32[]{:S(2)}, u32[]{:S(2)}) collective-permute-start(bf16[8,2,128,128]{3,2,1,0:T(8,128)(2,1)S(1)} %all_to_all.19.y_ref), channel_id=1, source_target_pairs={{0,512},{512,0},{1,513},{513,1},{2,514},{514,2},{3,515},{515,3},{4... | collective-permute-start | bytes 1572872 | tf_op jit(solution)/shard_map/ppermute | solution.py:114
  30.1 1.9 %collective-permute-start.1 = (bf16[8,2,128,128]{3,2,1,0:T(8,128)(2,1)S(1)}, bf16[8,2,128,128]{3,2,1,0:T(8,128)(2,1)S(1)}, u32[]{:S(2)}, u32[]{:S(2)}) collective-permute-start(bf16[8,2,128,128]{3,2,1,0:T(8,128)(2,1)S(1)} %all_to_all.19.y_ref), channel_id=1, source_target_pairs={{0,32},{32,0},{1,33},{33,1},{2,34},{34,2},{3,35},{35,3},{4,36},{36... | collective-permute-start | bytes 1572872 | tf_op jit(solution)/shard_map/ppermute | solution.py:115
  32.1 7.4 %collective-permute-done.z_ref = bf16[8,2,128,128]{3,2,1,0:T(8,128)(2,1)S(1)} collective-permute-done((bf16[8,2,128,128]{3,2,1,0:T(8,128)(2,1)S(1)}, bf16[8,2,128,128]{3,2,1,0:T(8,128)(2,1)S(1)}, u32[]{:S(2)}, u32[]{:S(2)}) %collective-permute-start) | collective-permute-done | bytes 524320 | tf_op jit(solution)/shard_map/ppermute | solution.py:114
  39.5 1.9 %collective-permute-start.2 = (bf16[8,2,128,128]{3,2,1,0:T(8,128)(2,1)S(1)}, bf16[8,2,128,128]{3,2,1,0:T(8,128)(2,1)S(1)}, u32[]{:S(2)}, u32[]{:S(2)}) collective-permute-start(bf16[8,2,128,128]{3,2,1,0:T(8,128)(2,1)S(1)} %collective-permute-done.z_ref), channel_id=1, source_target_pairs={{0,32},{32,0},{1,33},{33,1},{2,34},{34,2},{3,35},{35,3},{4,36},{36... | collective-permute-start | bytes 1572872 | tf_op jit(solution)/shard_map/ppermute | solution.py:116
  41.4 0.1 pad_add_fusion.place
  41.5 0.0 collective-permute-done.1.cy_ref
  41.5 1.8 %collective-permute-done.2.cz_ref = bf16[8,2,128,128]{3,2,1,0:T(8,128)(2,1)S(1)} collective-permute-done((bf16[8,2,128,128]{3,2,1,0:T(8,128)(2,1)S(1)}, bf16[8,2,128,128]{3,2,1,0:T(8,128)(2,1)S(1)}, u32[]{:S(2)}, u32[]{:S(2)}) %collective-permute-start.2) | collective-permute-done | bytes 524320 | tf_op jit(solution)/shard_map/ppermute | solution.py:116
  43.3 0.7 copy-done
  44.0 0.7 copy-done.1
  44.6 9.9 %terms.1 = (f32[16,16,512]{2,1,0:T(8,128)S(1)}, f32[16,16,512]{2,1,0:T(8,128)S(1)}) custom-call(s32[3]{0:T(128)S(1)} %pad_add_fusion.place, f32[3]{0:T(128)S(1)} %copy-done.1, bf16[8,2,128,128]{3,2,1,0:T(8,128)(2,1)S(1)} %all_to_all.19.y_ref, bf16[8,2,128,128]{3,2,1,0:T(8,128)(2,1)S(1)} %collective-permute-done.z_ref, ...), custom_call_target="tpu_custom_call" | custom-call | flops 3221225472 | bytes 12582912 | tf_op jit(solution)/shard_map/terms/pallas_call | solution.py:78
  54.5 2.0 %collective-permute-start.3 = (f32[16,16,512]{2,1,0:T(8,128)S(1)}, f32[16,16,512]{2,1,0:T(8,128)S(1)}, u32[]{:S(2)}, u32[]{:S(2)}) collective-permute-start(f32[16,16,512]{2,1,0:T(8,128)S(1)} %get-tuple-element.8), channel_id=1, source_target_pairs={{0,32},{32,0},{1,33},{33,1},{2,34},{34,2},{3,35},{35,3},{4,36},{36... | collective-permute-start | bytes 1572872 | tf_op jit(solution)/shard_map/ppermute | solution.py:118
  56.6 1.8 %collective-permute-done.3 = f32[16,16,512]{2,1,0:T(8,128)S(1)} collective-permute-done((f32[16,16,512]{2,1,0:T(8,128)S(1)}, f32[16,16,512]{2,1,0:T(8,128)S(1)}, u32[]{:S(2)}, u32[]{:S(2)}) %collective-permute-start.3) | collective-permute-done | bytes 524320 | tf_op jit(solution)/shard_map/ppermute | solution.py:118
  58.3 0.1 add_convert_fusion
  58.4 16.3 %all_to_all.20 = bf16[16,16,512]{2,1,0:T(8,128)(2,1)S(1)} all-to-all(bf16[16,16,512]{2,1,0:T(8,128)(2,1)S(1)} %add_convert_fusion), channel_id=1, replica_groups=mesh['zl'=2,'y'=8,'c'=2,'zh'=4,'x'=8] {'zl','y'}, dimensions={0} | all-to-all | bytes 524288 | tf_op jit(solution)/shard_map/all_to_all | solution.py:119
  74.8 0.1 reshape.19
  74.9 0.1 copy.10
  75.0 0.1 copy.11
  75.1 32.4 %all_to_all.21 = f32[32,1,256]{2,1,0:T(1,128)S(1)} all-to-all(f32[32,1,256]{2,1,0:T(1,128)S(1)} %copy.11), channel_id=1, replica_groups=mesh['zl'=2,'y'=8,'c'=2,'zh'=4,'x'=8] {'zh','x'}, dimensions={0} | all-to-all | bytes 65536 | tf_op jit(solution)/shard_map/all_to_all | solution.py:125
  107.6 0.1 reduce_sum.19
  107.6 0.7 mul.15
  (4 shorter events, 0.1 us)
Async XLA Ops:
  28.2 11.3 %collective-permute-start = (bf16[8,2,128,128]{3,2,1,0:T(8,128)(2,1)S(1)}, bf16[8,2,128,128]{3,2,1,0:T(8,128)(2,1)S(1)}, u32[]{:S(2)}, u32[]{:S(2)}) collective-permute-start(bf16[8,2,128,128]{3,2,1,0:T(8,128)(2,1)S(1)} %all_to_all.19.y_ref), channel_id=1, source_target_pairs={{0,512},{512,0},{1,513},{513,1},{2,514},{514,2},{3,515},{515,3},{4... | collective-permute-start | bytes 1572872 | tf_op jit(solution)/shard_map/ppermute | solution.py:114
  30.1 11.4 %collective-permute-start.1 = (bf16[8,2,128,128]{3,2,1,0:T(8,128)(2,1)S(1)}, bf16[8,2,128,128]{3,2,1,0:T(8,128)(2,1)S(1)}, u32[]{:S(2)}, u32[]{:S(2)}) collective-permute-start(bf16[8,2,128,128]{3,2,1,0:T(8,128)(2,1)S(1)} %all_to_all.19.y_ref), channel_id=1, source_target_pairs={{0,32},{32,0},{1,33},{33,1},{2,34},{34,2},{3,35},{35,3},{4,36},{36... | collective-permute-start | bytes 1572872 | tf_op jit(solution)/shard_map/ppermute | solution.py:115
  39.5 3.8 %collective-permute-start.2 = (bf16[8,2,128,128]{3,2,1,0:T(8,128)(2,1)S(1)}, bf16[8,2,128,128]{3,2,1,0:T(8,128)(2,1)S(1)}, u32[]{:S(2)}, u32[]{:S(2)}) collective-permute-start(bf16[8,2,128,128]{3,2,1,0:T(8,128)(2,1)S(1)} %collective-permute-done.z_ref), channel_id=1, source_target_pairs={{0,32},{32,0},{1,33},{33,1},{2,34},{34,2},{3,35},{35,3},{4,36},{36... | collective-permute-start | bytes 1572872 | tf_op jit(solution)/shard_map/ppermute | solution.py:116
  43.3 0.7 copy-start
  44.0 0.7 copy-start.1
  54.5 3.8 %collective-permute-start.3 = (f32[16,16,512]{2,1,0:T(8,128)S(1)}, f32[16,16,512]{2,1,0:T(8,128)S(1)}, u32[]{:S(2)}, u32[]{:S(2)}) collective-permute-start(f32[16,16,512]{2,1,0:T(8,128)S(1)} %get-tuple-element.8), channel_id=1, source_target_pairs={{0,32},{32,0},{1,33},{33,1},{2,34},{34,2},{3,35},{35,3},{4,36},{36... | collective-permute-start | bytes 1572872 | tf_op jit(solution)/shard_map/ppermute | solution.py:118

commit v2 on v1

v2 whole, which is shorter than its diff:
```python
import jax
import jax.numpy as jnp
from jax import lax
from jax.experimental import pallas as pl
from jax.experimental.pallas import tpu as pltpu
from jax.sharding import Mesh, PartitionSpec as P


CLASSES = 3
FINE = 16
F32 = jnp.float32
BF16 = jnp.bfloat16
VMEM = pl.BlockSpec(memory_space=pltpu.VMEM)


def prepare_body(energy, amps_ref, freqs_ref, class_ref, own_ref, square_ref, kind_ref):
    amps = amps_ref[...].astype(F32).T.astype(BF16)
    freqs = freqs_ref[...].astype(F32).T.astype(BF16)
    for k in range(own_ref.shape[0]):
        own_ref[k, 0] = amps
        own_ref[k, 1] = freqs
    for c in range(CLASSES):
        square_ref[c] = jnp.full(square_ref.shape[1:], energy[c] * energy[c], F32)
    kind_ref[...] = class_ref[...]


def prepare(screened, poles, gap_energy, gap_class, copies):
    rows, columns = screened.shape
    return pl.pallas_call(
        prepare_body,
        out_shape=(
            jax.ShapeDtypeStruct((copies, 2, columns, rows), BF16),
            jax.ShapeDtypeStruct((CLASSES, 8, rows), F32),
            jax.ShapeDtypeStruct(gap_class.shape, jnp.int32),
        ),
        grid=(1,),
        in_specs=[
            pl.BlockSpec(memory_space=pltpu.SMEM),
            pl.BlockSpec(screened.shape, lambda t: (0, 0)),
            pl.BlockSpec(poles.shape, lambda t: (0, 0)),
            pl.BlockSpec(gap_class.shape, lambda t: (0, 0)),
        ],
        out_specs=(VMEM, VMEM, VMEM),
        compiler_params=pltpu.CompilerParams(vmem_limit_bytes=8 << 20),
        name="prepare",
    )(*(pltpu.with_memory_space_constraint(a, pltpu.HBM) for a in (gap_energy, screened, poles, gap_class)))


def add_block(group, start, square_ref, inter_ref, acc):
    bands, blocks, size, states = inter_ref.shape
    squares = [square_ref[c, 0:1, :] for c in range(CLASSES)]
    columns = [[] for _ in range(CLASSES)]
    for j in range(blocks):
        amps = group[start + j, 0].astype(F32)
        freqs = group[start + j, 1].astype(F32)
        square = freqs * freqs
        d0, d1, d2 = (square + e for e in squares)
        d12 = d1 * d2
        ratio = amps * freqs / (d0 * d12)
        r0 = ratio * d0
        columns[0].append((ratio * d12).astype(BF16))
        columns[1].append((r0 * d2).astype(BF16))
        columns[2].append((r0 * d1).astype(BF16))
    factor = jnp.concatenate([jnp.concatenate(c, axis=1) for c in columns], axis=0)
    for b in range(bands):
        rows = inter_ref[b].reshape(blocks * size, states)
        acc[b] += jnp.dot(factor, rows, preferred_element_type=F32)


def first_body(place, square_ref, y_ref, cy_ref, inter_ref, acc):
    step = pl.program_id(0)
    start = lax.rem(step, 2) * inter_ref.shape[1]

    @pl.when(step == 0)
    def _():
        acc[...] = jnp.zeros_like(acc)

    pl.when(step // 2 == 0)(lambda: add_block(y_ref, start, square_ref, inter_ref, acc))
    pl.when(step // 2 == 1)(lambda: add_block(cy_ref, start, square_ref, inter_ref, acc))


def second_body(place, square_ref, z_ref, inter_ref, acc_in, acc):
    @pl.when(pl.program_id(0) == 0)
    def _():
        acc[...] = acc_in[...]

    add_block(z_ref, pl.program_id(0) * inter_ref.shape[1], square_ref, inter_ref, acc)


def third_body(place, square_ref, kind_ref, cz_ref, inter_ref, right_ref, acc_in, keep_ref, send_ref, acc, full):
    step = pl.program_id(0)
    bands, _, size, states = inter_ref.shape

    @pl.when(step == 0)
    def _():
        acc[...] = acc_in[...]

    add_block(cz_ref, step * inter_ref.shape[1], square_ref, inter_ref, acc)

    @pl.when(step == pl.num_programs(0) - 1)
    def _():
        sides = []
        for b in range(bands):
            kind = kind_ref[b : b + 1, :]
            side = jnp.zeros((size, states), F32)
            for c in range(CLASSES):
                side = jnp.where(kind == c, acc[b, c * size : (c + 1) * size, :], side)
            sides.append(side.astype(BF16))
        left = jnp.concatenate(sides, axis=0)
        right = right_ref[...].reshape(bands * size, states)
        total = lax.dot_general(left, right, (((0,), (0,)), ((), ())), preferred_element_type=F32)
        full[...] = total.reshape(full.shape)
        core = place[1]
        keep_ref[...] = full[:, core]
        send_ref[...] = full[:, 1 - core]


class Terms:
    def __init__(self, place, square, kind, intersections, per, size):
        bands, rows, states = intersections.shape
        self.place, self.square, self.kind = place, square, kind
        self.split = intersections.reshape(bands, 2, per, 2, size, states)
        self.flat = intersections.reshape(bands, rows // size, size, states)
        self.blocks = per // 2
        self.size = size
        self.acc = jax.ShapeDtypeStruct((bands, CLASSES * size, states), F32)

    def rows_spec(self, other_z, other_core):
        bands, _, _, _, size, states = self.split.shape

        def index(t, place):
            c = place[1] if other_core == 0 else 1 - place[1]
            c = c if other_core < 2 else lax.rem(place[1] + t // 2, 2)
            return (0, lax.rem(place[0] + other_z, 2), lax.rem(t, 2), c, 0, 0)

        return pl.BlockSpec((bands, None, self.blocks, None, size, states), index)

    def call(self, body, steps, operands, specs, out_shape, scratch=()):
        flops = 2 * self.acc.shape[0] * self.acc.shape[1] * self.acc.shape[2] * steps * self.blocks * self.size
        return pl.pallas_call(
            body,
            out_shape=out_shape,
            grid_spec=pltpu.PrefetchScalarGridSpec(
                num_scalar_prefetch=1,
                grid=(steps,),
                in_specs=specs,
                out_specs=VMEM if not isinstance(out_shape, tuple) else tuple(VMEM for _ in out_shape),
                scratch_shapes=scratch,
            ),
            compiler_params=pltpu.CompilerParams(dimension_semantics=("arbitrary",), vmem_limit_bytes=50 << 20),
            cost_estimate=pl.CostEstimate(flops=flops, bytes_accessed=steps << 20, transcendentals=0),
        )(self.place, *operands)

    def first(self, y_group, cy_group):
        return self.call(
            first_body, 4,
            (self.square, y_group, cy_group, self.split),
            [VMEM, VMEM, VMEM, self.rows_spec(0, 2)],
            self.acc,
        )

    def second(self, z_group, acc):
        return self.call(
            second_body, 2,
            (self.square, z_group, self.split, acc),
            [VMEM, VMEM, self.rows_spec(1, 0), VMEM],
            self.acc,
        )

    def third(self, cz_group, acc):
        bands, size, states = acc.shape[0], self.size, acc.shape[2]
        outer = states // (2 * FINE)
        half = jax.ShapeDtypeStruct((outer, FINE, states), F32)
        right = pl.BlockSpec((bands, None, size, states), lambda t, place: (0, place[2], 0, 0))
        return self.call(
            third_body, 2,
            (self.square, self.kind, cz_group, self.split, self.flat, acc),
            [VMEM, VMEM, VMEM, self.rows_spec(1, 1), right, VMEM],
            (half, half),
            [pltpu.VMEM(self.acc.shape, F32), pltpu.VMEM((outer, 2, FINE, states), F32)],
        )


def local(intersections, screened, poles, gap_energy, gap_class):
    zl, c = lax.axis_index("zl"), lax.axis_index("c")
    column = lax.axis_index("zh") * lax.axis_size("x") + lax.axis_index("x")
    place = jnp.stack([zl, c, column]).astype(jnp.int32)
    swap = [(0, 1), (1, 0)]
    per = lax.axis_size("y")
    own, square, kind = prepare(screened, poles, gap_energy, gap_class, per)
    terms = Terms(place, square, kind, intersections, per, screened.shape[0])
    y_group = lax.all_to_all(own, "y", 0, 0, tiled=True)
    z_group = lax.ppermute(y_group, "zl", swap)
    cy_group = lax.ppermute(y_group, "c", swap)
    acc = terms.first(y_group, cy_group)
    cz_group = lax.ppermute(z_group, "c", swap)
    acc = terms.second(z_group, acc)
    keep, send = terms.third(cz_group, acc)
    chip = keep + lax.ppermute(send, "c", swap)
    pieces = lax.all_to_all(chip.astype(BF16), ("zl", "y"), 0, 0, tiled=True)
    rows = jnp.sum(pieces.astype(F32), axis=0)
    columns = lax.axis_size("zh") * lax.axis_size("x")
    fine = rows.shape[0]
    split = rows.reshape(fine, columns, -1).transpose(1, 0, 2)
    wide = split.shape[2]
    blocks = lax.all_to_all(split.reshape(columns, fine * wide), ("zh", "x"), 0, 0, tiled=True)
    total = jnp.sum(blocks, axis=0).reshape(fine, wide)
    count = intersections.shape[1] * intersections.shape[0] * 2 * per * 2
    return total * (1.0 / jnp.sqrt(F32(count)))


def solution(mesh):
    fine = Mesh(mesh.devices.reshape(2, 8, 2, 4, 8), ("zl", "y", "c", "zh", "x"))
    band, col = ("zl", "y", "c"), ("zh", "x")
    return jax.shard_map(
        local,
        mesh=fine,
        in_specs=(P(band, None, None), P(band, col), P(band, col), P(), P(band, None)),
        out_specs=P(band, col),
        check_vma=False,
    )
```

time: 109 us -> 108 us (level)
  Pallas kernels: 9.88 us -> 12.9 us
  waiting for transfers between devices: 11 us -> 8.96 us
  local copies, waits for them, and re-layouts: 2.56 us -> 1 us
    pallas_call x1 -> x4, Pallas kernels: 9.88 us -> 12.9 us  [the longest x3 12 us: call(): pl.pallas_call(body, out_shape=out_shape, grid_spec=pltpu.PrefetchScalarG...]
    ppermute x1, waiting for transfers between devices: 1.79 us -> 0.01 us  [local(): cz_group = lax.ppermute(z_group, 'c', swap)]
    unnamed x4 -> x0, local copies, waits for them, and re-layouts: 1.34 us -> none
  transfers between devices with their start and end apart: 4 -> 4, of which waited for: 3 -> 2; matrix products, arithmetic and copies ran while one was open for 0% -> 0% of each run, Pallas kernels for 0% -> 8%
where the time goes in v2:
time: 108 us
  blocking collectives  76.3 us (71%)
  Pallas kernels  12.9 us (12%)
  waiting for transfers between devices  8.96 us (8%)
  starting transfers between devices  8.15 us (8%)
    all_to_all x1, blocking collectives, local(): lax.all_to_all(split.reshape(columns, fine * wide), ('zh', 'x'), 0, 0, ti...  32.4 us
    all_to_all x1, blocking collectives, local(): y_group = lax.all_to_all(own, 'y', 0, 0, tiled=True)  27.2 us
    all_to_all x1, blocking collectives, local(): pieces = lax.all_to_all(chip.astype(BF16), ('zl', 'y'), 0, 0, tiled=True)  16.7 us
    pallas_call x3, Pallas kernels, call(): pl.pallas_call(body, out_shape=out_shape, grid_spec=pltpu.PrefetchScalarG...  12 us
    ppermute x1, waiting for transfers between devices, local(): z_group = lax.ppermute(y_group, 'zl', swap)  7.44 us
    ppermute x1, starting transfers between devices, local(): chip = keep + lax.ppermute(send, 'c', swap)  2.41 us
  transfers between devices with their start and end apart: 4, of which 2 were waited for; matrix products, arithmetic and copies ran while one was open for 0% of the time, Pallas kernels for 8%

profile of v2, /device:TPU:16, one launch (start us, length us, event | category | flops | bytes accessed | tf_op | source)
XLA Modules:
  0.0 107.7 jit_solution(3172996158722281567)
XLA Ops:
  0.0 0.9 prepare.1
  0.9 27.2 %all_to_all.19.y_ref = bf16[8,2,128,128]{3,2,1,0:T(8,128)(2,1)S(1)} all-to-all(bf16[8,2,128,128]{3,2,1,0:T(8,128)(2,1)S(1)} %get-tuple-element.12), channel_id=1, replica_groups=mesh['zl'=2,'y'=8,'c'=2,'zh'=4,'x'=8] {'y'}, dimensions={0} | all-to-all | bytes 1048576 | tf_op jit(solution)/shard_map/all_to_all | solution.py:192
  28.1 1.9 %collective-permute-start = (bf16[8,2,128,128]{3,2,1,0:T(8,128)(2,1)S(1)}, bf16[8,2,128,128]{3,2,1,0:T(8,128)(2,1)S(1)}, u32[]{:S(2)}, u32[]{:S(2)}) collective-permute-start(bf16[8,2,128,128]{3,2,1,0:T(8,128)(2,1)S(1)} %all_to_all.19.y_ref), channel_id=1, source_target_pairs={{0,512},{512,0},{1,513},{513,1},{2,514},{514,2},{3,515},{515,3},{4... | collective-permute-start | bytes 1572872 | tf_op jit(solution)/shard_map/ppermute | solution.py:193
  30.0 1.9 %collective-permute-start.2 = (bf16[8,2,128,128]{3,2,1,0:T(8,128)(2,1)S(1)}, bf16[8,2,128,128]{3,2,1,0:T(8,128)(2,1)S(1)}, u32[]{:S(2)}, u32[]{:S(2)}) collective-permute-start(bf16[8,2,128,128]{3,2,1,0:T(8,128)(2,1)S(1)} %all_to_all.19.y_ref), channel_id=1, source_target_pairs={{0,32},{32,0},{1,33},{33,1},{2,34},{34,2},{3,35},{35,3},{4,36},{36... | collective-permute-start | bytes 1572872 | tf_op jit(solution)/shard_map/ppermute | solution.py:194
  32.0 7.4 %collective-permute-done.z_ref = bf16[8,2,128,128]{3,2,1,0:T(8,128)(2,1)S(1)} collective-permute-done((bf16[8,2,128,128]{3,2,1,0:T(8,128)(2,1)S(1)}, bf16[8,2,128,128]{3,2,1,0:T(8,128)(2,1)S(1)}, u32[]{:S(2)}, u32[]{:S(2)}) %collective-permute-start) | collective-permute-done | bytes 524320 | tf_op jit(solution)/shard_map/ppermute | solution.py:193
  39.4 1.9 %collective-permute-start.1 = (bf16[8,2,128,128]{3,2,1,0:T(8,128)(2,1)S(1)}, bf16[8,2,128,128]{3,2,1,0:T(8,128)(2,1)S(1)}, u32[]{:S(2)}, u32[]{:S(2)}) collective-permute-start(bf16[8,2,128,128]{3,2,1,0:T(8,128)(2,1)S(1)} %collective-permute-done.z_ref), channel_id=1, source_target_pairs={{0,32},{32,0},{1,33},{33,1},{2,34},{34,2},{3,35},{35,3},{4,36},{36... | collective-permute-start | bytes 1572872 | tf_op jit(solution)/shard_map/ppermute | solution.py:196
  41.3 0.1 pad_add_fusion.place
  41.4 0.0 collective-permute-done.2.cy_ref
  41.4 5.2 %shard_map.55.acc_in = f32[2,384,512]{2,1,0:T(8,128)S(1)} custom-call(s32[3]{0:T(128)S(1)} %pad_add_fusion.place, f32[3,8,128]{2,1,0:T(8,128)S(1)} %get-tuple-element.10.square_ref, bf16[8,2,128,128]{3,2,1,0:T(8,128)(2,1)S(1)} %all_to_all.19.y_ref, bf16[8,2,128,128]{3,2,1,0:T(8,128)(2,1)S(1)} %collective-permute-done.2.cy_ref, ...), custom_call_target="tpu_custom_call" | custom-call | flops 1610612736 | bytes 4194304 | tf_op jit(solution)/shard_map/pallas_call | solution.py:140
  46.6 3.2 %shard_map.56.acc_in = f32[2,384,512]{2,1,0:T(8,128)S(1)} custom-call(s32[3]{0:T(128)S(1)} %pad_add_fusion.place, f32[3,8,128]{2,1,0:T(8,128)S(1)} %get-tuple-element.10.square_ref, bf16[8,2,128,128]{3,2,1,0:T(8,128)(2,1)S(1)} %collective-permute-done.z_ref, bf16[2,2,8,2,128,512]{5,4,3,2,1,0:T(8,128)(2,1)} %bitcast.8, f32[2,384,512]{2,1,0:T(8,128)S(1)} %shard_map.55.acc_in), custom_call_target="tpu_custom_call" | custom-call | flops 805306368 | bytes 2097152 | tf_op jit(solution)/shard_map/pallas_call | solution.py:140
  49.7 0.0 collective-permute-done.1.cz_ref
  49.8 3.7 %shard_map.57 = (f32[16,16,512]{2,1,0:T(8,128)S(1)}, f32[16,16,512]{2,1,0:T(8,128)S(1)}) custom-call(s32[3]{0:T(128)S(1)} %pad_add_fusion.place, f32[3,8,128]{2,1,0:T(8,128)S(1)} %get-tuple-element.10.square_ref, s32[2,512]{1,0:T(2,128)S(1)} %get-tuple-element.11.kind_ref, bf16[8,2,128,128]{3,2,1,0:T(8,128)(2,1)S(1)} %collective-permute-done.1.cz_ref, ...), custom_call_target="tpu_custom_call" | custom-call | flops 805306368 | bytes 2097152 | tf_op jit(solution)/shard_map/pallas_call | solution.py:140
  53.4 2.4 %collective-permute-start.3 = (f32[16,16,512]{2,1,0:T(8,128)S(1)}, f32[16,16,512]{2,1,0:T(8,128)S(1)}, u32[]{:S(2)}, u32[]{:S(2)}) collective-permute-start(f32[16,16,512]{2,1,0:T(8,128)S(1)} %get-tuple-element.14), channel_id=1, source_target_pairs={{0,32},{32,0},{1,33},{33,1},{2,34},{34,2},{3,35},{35,3},{4,36},{36... | collective-permute-start | bytes 1572872 | tf_op jit(solution)/shard_map/ppermute | solution.py:199
  55.8 1.5 %collective-permute-done.3 = f32[16,16,512]{2,1,0:T(8,128)S(1)} collective-permute-done((f32[16,16,512]{2,1,0:T(8,128)S(1)}, f32[16,16,512]{2,1,0:T(8,128)S(1)}, u32[]{:S(2)}, u32[]{:S(2)}) %collective-permute-start.3) | collective-permute-done | bytes 524320 | tf_op jit(solution)/shard_map/ppermute | solution.py:199
  57.4 0.1 add_convert_fusion
  57.5 16.7 %all_to_all.20 = bf16[16,16,512]{2,1,0:T(8,128)(2,1)S(1)} all-to-all(bf16[16,16,512]{2,1,0:T(8,128)(2,1)S(1)} %add_convert_fusion), channel_id=1, replica_groups=mesh['zl'=2,'y'=8,'c'=2,'zh'=4,'x'=8] {'zl','y'}, dimensions={0} | all-to-all | bytes 524288 | tf_op jit(solution)/shard_map/all_to_all | solution.py:200
  74.2 0.1 reshape.18
  74.3 0.1 copy.7
  74.4 0.1 copy.8
  74.5 32.4 %all_to_all.21 = f32[32,1,256]{2,1,0:T(1,128)S(1)} all-to-all(f32[32,1,256]{2,1,0:T(1,128)S(1)} %copy.8), channel_id=1, replica_groups=mesh['zl'=2,'y'=8,'c'=2,'zh'=4,'x'=8] {'zh','x'}, dimensions={0} | all-to-all | bytes 65536 | tf_op jit(solution)/shard_map/all_to_all | solution.py:206
  106.9 0.1 reduce_sum.19
  107.0 0.7 mul.15
  (2 shorter events, 0.0 us)
Async XLA Ops:
  28.1 11.3 %collective-permute-start = (bf16[8,2,128,128]{3,2,1,0:T(8,128)(2,1)S(1)}, bf16[8,2,128,128]{3,2,1,0:T(8,128)(2,1)S(1)}, u32[]{:S(2)}, u32[]{:S(2)}) collective-permute-start(bf16[8,2,128,128]{3,2,1,0:T(8,128)(2,1)S(1)} %all_to_all.19.y_ref), channel_id=1, source_target_pairs={{0,512},{512,0},{1,513},{513,1},{2,514},{514,2},{3,515},{515,3},{4... | collective-permute-start | bytes 1572872 | tf_op jit(solution)/shard_map/ppermute | solution.py:193
  30.0 11.4 %collective-permute-start.2 = (bf16[8,2,128,128]{3,2,1,0:T(8,128)(2,1)S(1)}, bf16[8,2,128,128]{3,2,1,0:T(8,128)(2,1)S(1)}, u32[]{:S(2)}, u32[]{:S(2)}) collective-permute-start(bf16[8,2,128,128]{3,2,1,0:T(8,128)(2,1)S(1)} %all_to_all.19.y_ref), channel_id=1, source_target_pairs={{0,32},{32,0},{1,33},{33,1},{2,34},{34,2},{3,35},{35,3},{4,36},{36... | collective-permute-start | bytes 1572872 | tf_op jit(solution)/shard_map/ppermute | solution.py:194
  39.4 10.3 %collective-permute-start.1 = (bf16[8,2,128,128]{3,2,1,0:T(8,128)(2,1)S(1)}, bf16[8,2,128,128]{3,2,1,0:T(8,128)(2,1)S(1)}, u32[]{:S(2)}, u32[]{:S(2)}) collective-permute-start(bf16[8,2,128,128]{3,2,1,0:T(8,128)(2,1)S(1)} %collective-permute-done.z_ref), channel_id=1, source_target_pairs={{0,32},{32,0},{1,33},{33,1},{2,34},{34,2},{3,35},{35,3},{4,36},{36... | collective-permute-start | bytes 1572872 | tf_op jit(solution)/shard_map/ppermute | solution.py:196
  53.4 3.9 %collective-permute-start.3 = (f32[16,16,512]{2,1,0:T(8,128)S(1)}, f32[16,16,512]{2,1,0:T(8,128)S(1)}, u32[]{:S(2)}, u32[]{:S(2)}) collective-permute-start(f32[16,16,512]{2,1,0:T(8,128)S(1)} %get-tuple-element.14), channel_id=1, source_target_pairs={{0,32},{32,0},{1,33},{33,1},{2,34},{34,2},{3,35},{35,3},{4,36},{36... | collective-permute-start | bytes 1572872 | tf_op jit(solution)/shard_map/ppermute | solution.py:199

commit v3 on v2

v3 whole, which is shorter than its diff:
```python
import jax
import jax.numpy as jnp
from jax import lax
from jax.experimental import pallas as pl
from jax.experimental.pallas import tpu as pltpu
from jax.sharding import Mesh, PartitionSpec as P


CLASSES = 3
FINE = 16
LIMIT = 32 << 20
F32 = jnp.float32
BF16 = jnp.bfloat16
VMEM = pl.BlockSpec(memory_space=pltpu.VMEM)


def prepare_body(energy, amps_ref, freqs_ref, class_ref, own_ref, square_ref, kind_ref):
    amps = amps_ref[...].astype(F32).T.astype(BF16)
    freqs = freqs_ref[...].astype(F32).T.astype(BF16)
    for k in range(own_ref.shape[0]):
        own_ref[k, 0] = amps
        own_ref[k, 1] = freqs
    for c in range(CLASSES):
        square_ref[c] = jnp.full(square_ref.shape[1:], energy[c] * energy[c], F32)
    kind_ref[...] = class_ref[...]


def prepare(screened, poles, gap_energy, gap_class, copies):
    rows, columns = screened.shape
    return pl.pallas_call(
        prepare_body,
        out_shape=(
            jax.ShapeDtypeStruct((copies, 2, columns, rows), BF16),
            jax.ShapeDtypeStruct((CLASSES, 8, rows), F32),
            jax.ShapeDtypeStruct(gap_class.shape, jnp.int32),
        ),
        grid=(1,),
        in_specs=[
            pl.BlockSpec(memory_space=pltpu.SMEM),
            pl.BlockSpec(screened.shape, lambda t: (0, 0)),
            pl.BlockSpec(poles.shape, lambda t: (0, 0)),
            pl.BlockSpec(gap_class.shape, lambda t: (0, 0)),
        ],
        out_specs=(VMEM, VMEM, VMEM),
        compiler_params=pltpu.CompilerParams(vmem_limit_bytes=8 << 20),
        name="prepare",
    )(*(pltpu.with_memory_space_constraint(a, pltpu.HBM) for a in (gap_energy, screened, poles, gap_class)))


def factors(group, start, blocks, square_ref):
    squares = [square_ref[c, 0:1, :] for c in range(CLASSES)]
    columns = [[] for _ in range(CLASSES)]
    for j in range(blocks):
        amps = group[start + j, 0].astype(F32)
        freqs = group[start + j, 1].astype(F32)
        square = freqs * freqs
        d0, d1, d2 = (square + e for e in squares)
        d12 = d1 * d2
        ratio = amps * freqs / (d0 * d12)
        r0 = ratio * d0
        columns[0].append((ratio * d12).astype(BF16))
        columns[1].append((r0 * d2).astype(BF16))
        columns[2].append((r0 * d1).astype(BF16))
    return jnp.concatenate([jnp.concatenate(c, axis=1) for c in columns], axis=0)


def first_body(place, square_ref, y_ref, cy_ref, inter_ref, split_ref, flat_ref, acc, same_ref, cross_ref, right_ref, sems):
    step = pl.program_id(0)
    bands, blocks, size, states = inter_ref.shape
    other_z, core = 1 - place[0], place[1]
    copies = [
        pltpu.make_async_copy(split_ref.at[:, other_z, :, core], same_ref, sems.at[0]),
        pltpu.make_async_copy(split_ref.at[:, other_z, :, 1 - core], cross_ref, sems.at[1]),
        pltpu.make_async_copy(flat_ref.at[:, place[2]], right_ref, sems.at[2]),
    ]

    @pl.when(step == 0)
    def _():
        acc[...] = jnp.zeros_like(acc)

    @pl.when(step == 1)
    def _():
        for copy in copies:
            copy.start()

    def add(group):
        factor = factors(group, lax.rem(step, 2) * blocks, blocks, square_ref)
        for b in range(bands):
            rows = inter_ref[b].reshape(blocks * size, states)
            acc[b] += jnp.dot(factor, rows, preferred_element_type=F32)

    pl.when(step // 2 == 0)(lambda: add(y_ref))
    pl.when(step // 2 == 1)(lambda: add(cy_ref))

    @pl.when(step == pl.num_programs(0) - 1)
    def _():
        for copy in copies:
            copy.wait()


def second_body(square_ref, z_ref, inter_ref, acc_in, acc):
    bands, blocks, size, states = inter_ref.shape
    factor = factors(z_ref, 0, blocks, square_ref)
    for b in range(bands):
        rows = inter_ref[b].reshape(blocks * size, states)
        acc[b] = acc_in[b] + jnp.dot(factor, rows, preferred_element_type=F32)


def third_body(square_ref, kind_ref, cz_ref, inter_ref, right_ref, acc_in, keep_ref, send_ref, full):
    bands, blocks, size, states = inter_ref.shape
    factor = factors(cz_ref, 0, blocks, square_ref)
    sides = []
    for b in range(bands):
        rows = inter_ref[b].reshape(blocks * size, states)
        acc = acc_in[b] + jnp.dot(factor, rows, preferred_element_type=F32)
        kind = kind_ref[b : b + 1, :]
        side = jnp.zeros((size, states), F32)
        for c in range(CLASSES):
            side = jnp.where(kind == c, acc[c * size : (c + 1) * size, :], side)
        sides.append(side.astype(BF16))
    left = jnp.concatenate(sides, axis=0)
    right = right_ref[...].reshape(bands * size, states)
    total = lax.dot_general(left, right, (((0,), (0,)), ((), ())), preferred_element_type=F32)
    full[...] = total.reshape(full.shape)
    core = lax.axis_index("c")
    keep_ref[...] = full[:, core]
    send_ref[...] = full[:, 1 - core]


def work(acc, blocks, size, steps):
    flops = 2 * acc.shape[0] * acc.shape[1] * acc.shape[2] * blocks * size * steps
    return pl.CostEstimate(flops=flops, bytes_accessed=1 << 20, transcendentals=0)


def first(place, square, y_group, cy_group, intersections):
    bands, rows, states = intersections.shape
    per, size = y_group.shape[0], y_group.shape[3]
    blocks = per // 2
    split = pltpu.with_memory_space_constraint(intersections.reshape(bands, 2, per, 2, size, states), pltpu.HBM)
    flat = pltpu.with_memory_space_constraint(intersections.reshape(bands, rows // size, size, states), pltpu.HBM)
    acc = jax.ShapeDtypeStruct((bands, CLASSES * size, states), F32)
    half = jax.ShapeDtypeStruct((bands, per, size, states), BF16)
    right = jax.ShapeDtypeStruct((bands, size, states), BF16)

    def rows_of(t, place):
        return (0, place[0], lax.rem(t, 2), lax.rem(place[1] + t // 2, 2), 0, 0)

    return pl.pallas_call(
        first_body,
        out_shape=(acc, half, half, right),
        grid_spec=pltpu.PrefetchScalarGridSpec(
            num_scalar_prefetch=1,
            grid=(4,),
            in_specs=[
                VMEM,
                VMEM,
                VMEM,
                pl.BlockSpec((bands, None, blocks, None, size, states), rows_of),
                pl.BlockSpec(memory_space=pltpu.HBM),
                pl.BlockSpec(memory_space=pltpu.HBM),
            ],
            out_specs=(VMEM,) * 4,
            scratch_shapes=[pltpu.SemaphoreType.DMA((3,))],
        ),
        compiler_params=pltpu.CompilerParams(dimension_semantics=("arbitrary",), vmem_limit_bytes=LIMIT),
        cost_estimate=work(acc, blocks, size, 4),
        name="first",
    )(place, square, y_group, cy_group, split, split, flat)


def second(square, z_group, inter, acc):
    return pl.pallas_call(
        second_body,
        out_shape=jax.ShapeDtypeStruct(acc.shape, F32),
        in_specs=[VMEM] * 4,
        out_specs=VMEM,
        compiler_params=pltpu.CompilerParams(vmem_limit_bytes=LIMIT),
        cost_estimate=work(acc, *inter.shape[1:3], 1),
        name="second",
    )(square, z_group, inter, acc)


def third(square, kind, cz_group, inter, right, acc):
    outer, states = acc.shape[2] // (2 * FINE), acc.shape[2]
    half = jax.ShapeDtypeStruct((outer, FINE, states), F32)
    return pl.pallas_call(
        third_body,
        out_shape=(half, half),
        in_specs=[VMEM] * 6,
        out_specs=(VMEM, VMEM),
        scratch_shapes=[pltpu.VMEM((outer, 2, FINE, states), F32)],
        compiler_params=pltpu.CompilerParams(vmem_limit_bytes=LIMIT),
        cost_estimate=work(acc, *inter.shape[1:3], 1),
        name="third",
    )(square, kind, cz_group, inter, right, acc)


def local(intersections, screened, poles, gap_energy, gap_class):
    zl, c = lax.axis_index("zl"), lax.axis_index("c")
    column = lax.axis_index("zh") * lax.axis_size("x") + lax.axis_index("x")
    place = jnp.stack([zl, c, column]).astype(jnp.int32)
    swap = [(0, 1), (1, 0)]
    per = lax.axis_size("y")
    own, square, kind = prepare(screened, poles, gap_energy, gap_class, per)
    y_group = lax.all_to_all(own, "y", 0, 0, tiled=True)
    z_group = lax.ppermute(y_group, "zl", swap)
    cy_group = lax.ppermute(y_group, "c", swap)
    acc, same, cross, right = first(place, square, y_group, cy_group, intersections)
    cz_group = lax.ppermute(z_group, "c", swap)
    acc = second(square, z_group, same, acc)
    keep, send = third(square, kind, cz_group, cross, right, acc)
    chip = keep + lax.ppermute(send, "c", swap)
    pieces = lax.all_to_all(chip.astype(BF16), ("zl", "y"), 0, 0, tiled=True)
    rows = jnp.sum(pieces.astype(F32), axis=0)
    columns = lax.axis_size("zh") * lax.axis_size("x")
    fine = rows.shape[0]
    split = rows.reshape(fine, columns, -1).transpose(1, 0, 2)
    wide = split.shape[2]
    blocks = lax.all_to_all(split.reshape(columns, fine * wide), ("zh", "x"), 0, 0, tiled=True)
    total = jnp.sum(blocks, axis=0).reshape(fine, wide)
    count = intersections.shape[1] * intersections.shape[0] * 2 * per * 2
    return total * (1.0 / jnp.sqrt(F32(count)))


def solution(mesh):
    fine = Mesh(mesh.devices.reshape(2, 8, 2, 4, 8), ("zl", "y", "c", "zh", "x"))
    band, col = ("zl", "y", "c"), ("zh", "x")
    return jax.shard_map(
        local,
        mesh=fine,
        in_specs=(P(band, None, None), P(band, col), P(band, col), P(), P(band, None)),
        out_specs=P(band, col),
        check_vma=False,
    )
```

time: 108 us -> 105 us (0.972)
  Pallas kernels: 12.9 us -> 9.54 us
    pallas_call x3, Pallas kernels: 12 us -> 8.62 us  [the longest x1 6.24 us: first(): pl.pallas_call(first_body, out_shape=(acc, half, half, right), grid_spec=...]
  transfers between devices with their start and end apart: 4 -> 4, of which waited for: 2 -> 2; matrix products, arithmetic and copies ran while one was open for 0% -> 0% of each run, Pallas kernels for 8% -> 7%
where the time goes in v3:
time: 105 us; the launch traced here: 104 us
  blocking collectives  76.3 us (73%)
  Pallas kernels  9.54 us (9%)
  waiting for transfers between devices  8.96 us (9%)
  starting transfers between devices  8.18 us (8%)
    all_to_all x1, blocking collectives, local(): lax.all_to_all(split.reshape(columns, fine * wide), ('zh', 'x'), 0, 0, ti...  32.4 us
    all_to_all x1, blocking collectives, local(): y_group = lax.all_to_all(own, 'y', 0, 0, tiled=True)  27.2 us
    all_to_all x1, blocking collectives, local(): pieces = lax.all_to_all(chip.astype(BF16), ('zl', 'y'), 0, 0, tiled=True)  16.7 us
    ppermute x1, waiting for transfers between devices, local(): z_group = lax.ppermute(y_group, 'zl', swap)  7.44 us
    pallas_call x1, Pallas kernels, first(): pl.pallas_call(first_body, out_shape=(acc, half, half, right), grid_spec=...  6.24 us
    ppermute x1, starting transfers between devices, local(): chip = keep + lax.ppermute(send, 'c', swap)  2.44 us
  transfers between devices with their start and end apart: 4, of which 2 were waited for; matrix products, arithmetic and copies ran while one was open for 0% of the time, Pallas kernels for 7%

profile of v3, /device:TPU:16, one launch (start us, length us, event | category | flops | bytes accessed | tf_op | source)
XLA Modules:
  0.0 104.4 jit_solution(8919460210359413753)
XLA Ops:
  0.0 0.9 prepare.1
  0.9 27.2 %all_to_all.19.y_ref = bf16[8,2,128,128]{3,2,1,0:T(8,128)(2,1)S(1)} all-to-all(bf16[8,2,128,128]{3,2,1,0:T(8,128)(2,1)S(1)} %get-tuple-element.16), channel_id=1, replica_groups=mesh['zl'=2,'y'=8,'c'=2,'zh'=4,'x'=8] {'y'}, dimensions={0} | all-to-all | bytes 1048576 | tf_op jit(solution)/shard_map/all_to_all | solution.py:205
  28.1 1.9 %collective-permute-start = (bf16[8,2,128,128]{3,2,1,0:T(8,128)(2,1)S(1)}, bf16[8,2,128,128]{3,2,1,0:T(8,128)(2,1)S(1)}, u32[]{:S(2)}, u32[]{:S(2)}) collective-permute-start(bf16[8,2,128,128]{3,2,1,0:T(8,128)(2,1)S(1)} %all_to_all.19.y_ref), channel_id=1, source_target_pairs={{0,512},{512,0},{1,513},{513,1},{2,514},{514,2},{3,515},{515,3},{4... | collective-permute-start | bytes 1572872 | tf_op jit(solution)/shard_map/ppermute | solution.py:206
  30.0 1.9 %collective-permute-start.2 = (bf16[8,2,128,128]{3,2,1,0:T(8,128)(2,1)S(1)}, bf16[8,2,128,128]{3,2,1,0:T(8,128)(2,1)S(1)}, u32[]{:S(2)}, u32[]{:S(2)}) collective-permute-start(bf16[8,2,128,128]{3,2,1,0:T(8,128)(2,1)S(1)} %all_to_all.19.y_ref), channel_id=1, source_target_pairs={{0,32},{32,0},{1,33},{33,1},{2,34},{34,2},{3,35},{35,3},{4,36},{36... | collective-permute-start | bytes 1572872 | tf_op jit(solution)/shard_map/ppermute | solution.py:207
  32.0 7.4 %collective-permute-done.z_ref = bf16[8,2,128,128]{3,2,1,0:T(8,128)(2,1)S(1)} collective-permute-done((bf16[8,2,128,128]{3,2,1,0:T(8,128)(2,1)S(1)}, bf16[8,2,128,128]{3,2,1,0:T(8,128)(2,1)S(1)}, u32[]{:S(2)}, u32[]{:S(2)}) %collective-permute-start) | collective-permute-done | bytes 524320 | tf_op jit(solution)/shard_map/ppermute | solution.py:206
  39.4 1.9 %collective-permute-start.1 = (bf16[8,2,128,128]{3,2,1,0:T(8,128)(2,1)S(1)}, bf16[8,2,128,128]{3,2,1,0:T(8,128)(2,1)S(1)}, u32[]{:S(2)}, u32[]{:S(2)}) collective-permute-start(bf16[8,2,128,128]{3,2,1,0:T(8,128)(2,1)S(1)} %collective-permute-done.z_ref), channel_id=1, source_target_pairs={{0,32},{32,0},{1,33},{33,1},{2,34},{34,2},{3,35},{35,3},{4,36},{36... | collective-permute-start | bytes 1572872 | tf_op jit(solution)/shard_map/ppermute | solution.py:209
  41.3 0.1 pad_add_fusion.place
  41.4 0.0 collective-permute-done.2.cy_ref
  41.4 6.2 %first.1 = (f32[2,384,512]{2,1,0:T(8,128)S(1)}, bf16[2,8,128,512]{3,2,1,0:T(8,128)(2,1)S(1)}, bf16[2,8,128,512]{3,2,1,0:T(8,128)(2,1)S(1)}, bf16[2,128,512]{2,1,0:T(8,128)(2,1)S(1)}) custom-call(s32[3]{0:T(128)S(1)} %pad_add_fusion.place, f32[3,8,128]{2,1,0:T(8,128)S(1)} %get-tuple-element.14.square_ref, bf16[8,2,128,128]{3,2,1,0:T(8,128)(2,1)S(1)} %all_to_all.19.y_ref, ...), custom_call_target="tpu_custom_call" | custom-call | flops 1610612736 | bytes 1048576 | tf_op jit(solution)/shard_map/first/pallas_call | solution.py:148
  47.7 1.0 second.1.acc_in
  48.7 0.0 collective-permute-done.1.cz_ref
  48.7 1.4 %third.1 = (f32[16,16,512]{2,1,0:T(8,128)S(1)}, f32[16,16,512]{2,1,0:T(8,128)S(1)}) custom-call(f32[3,8,128]{2,1,0:T(8,128)S(1)} %get-tuple-element.14.square_ref, s32[2,512]{1,0:T(2,128)S(1)} %get-tuple-element.15.kind_ref, bf16[8,2,128,128]{3,2,1,0:T(8,128)(2,1)S(1)} %collective-permute-done.1.cz_ref, ...), custom_call_target="tpu_custom_call" | custom-call | flops 805306368 | bytes 1048576 | tf_op jit(solution)/shard_map/third/pallas_call | solution.py:186
  50.1 2.4 %collective-permute-start.3 = (f32[16,16,512]{2,1,0:T(8,128)S(1)}, f32[16,16,512]{2,1,0:T(8,128)S(1)}, u32[]{:S(2)}, u32[]{:S(2)}) collective-permute-start(f32[16,16,512]{2,1,0:T(8,128)S(1)} %get-tuple-element.22), channel_id=1, source_target_pairs={{0,32},{32,0},{1,33},{33,1},{2,34},{34,2},{3,35},{35,3},{4,36},{36... | collective-permute-start | bytes 1572872 | tf_op jit(solution)/shard_map/ppermute | solution.py:212
  52.5 1.5 %collective-permute-done.3 = f32[16,16,512]{2,1,0:T(8,128)S(1)} collective-permute-done((f32[16,16,512]{2,1,0:T(8,128)S(1)}, f32[16,16,512]{2,1,0:T(8,128)S(1)}, u32[]{:S(2)}, u32[]{:S(2)}) %collective-permute-start.3) | collective-permute-done | bytes 524320 | tf_op jit(solution)/shard_map/ppermute | solution.py:212
  54.0 0.1 add_convert_fusion
  54.1 16.7 %all_to_all.20 = bf16[16,16,512]{2,1,0:T(8,128)(2,1)S(1)} all-to-all(bf16[16,16,512]{2,1,0:T(8,128)(2,1)S(1)} %add_convert_fusion), channel_id=1, replica_groups=mesh['zl'=2,'y'=8,'c'=2,'zh'=4,'x'=8] {'zl','y'}, dimensions={0} | all-to-all | bytes 524288 | tf_op jit(solution)/shard_map/all_to_all | solution.py:213
  70.8 0.1 reshape.18
  71.0 0.1 copy.7
  71.1 0.1 copy.8
  71.2 32.4 %all_to_all.21 = f32[32,1,256]{2,1,0:T(1,128)S(1)} all-to-all(f32[32,1,256]{2,1,0:T(1,128)S(1)} %copy.8), channel_id=1, replica_groups=mesh['zl'=2,'y'=8,'c'=2,'zh'=4,'x'=8] {'zh','x'}, dimensions={0} | all-to-all | bytes 65536 | tf_op jit(solution)/shard_map/all_to_all | solution.py:219
  103.6 0.1 reduce_sum.19
  103.7 0.7 mul.15
  (2 shorter events, 0.0 us)
Async XLA Ops:
  28.1 11.3 %collective-permute-start = (bf16[8,2,128,128]{3,2,1,0:T(8,128)(2,1)S(1)}, bf16[8,2,128,128]{3,2,1,0:T(8,128)(2,1)S(1)}, u32[]{:S(2)}, u32[]{:S(2)}) collective-permute-start(bf16[8,2,128,128]{3,2,1,0:T(8,128)(2,1)S(1)} %all_to_all.19.y_ref), channel_id=1, source_target_pairs={{0,512},{512,0},{1,513},{513,1},{2,514},{514,2},{3,515},{515,3},{4... | collective-permute-start | bytes 1572872 | tf_op jit(solution)/shard_map/ppermute | solution.py:206
  30.0 11.4 %collective-permute-start.2 = (bf16[8,2,128,128]{3,2,1,0:T(8,128)(2,1)S(1)}, bf16[8,2,128,128]{3,2,1,0:T(8,128)(2,1)S(1)}, u32[]{:S(2)}, u32[]{:S(2)}) collective-permute-start(bf16[8,2,128,128]{3,2,1,0:T(8,128)(2,1)S(1)} %all_to_all.19.y_ref), channel_id=1, source_target_pairs={{0,32},{32,0},{1,33},{33,1},{2,34},{34,2},{3,35},{35,3},{4,36},{36... | collective-permute-start | bytes 1572872 | tf_op jit(solution)/shard_map/ppermute | solution.py:207
  39.4 9.3 %collective-permute-start.1 = (bf16[8,2,128,128]{3,2,1,0:T(8,128)(2,1)S(1)}, bf16[8,2,128,128]{3,2,1,0:T(8,128)(2,1)S(1)}, u32[]{:S(2)}, u32[]{:S(2)}) collective-permute-start(bf16[8,2,128,128]{3,2,1,0:T(8,128)(2,1)S(1)} %collective-permute-done.z_ref), channel_id=1, source_target_pairs={{0,32},{32,0},{1,33},{33,1},{2,34},{34,2},{3,35},{35,3},{4,36},{36... | collective-permute-start | bytes 1572872 | tf_op jit(solution)/shard_map/ppermute | solution.py:209
  50.1 4.0 %collective-permute-start.3 = (f32[16,16,512]{2,1,0:T(8,128)S(1)}, f32[16,16,512]{2,1,0:T(8,128)S(1)}, u32[]{:S(2)}, u32[]{:S(2)}) collective-permute-start(f32[16,16,512]{2,1,0:T(8,128)S(1)} %get-tuple-element.22), channel_id=1, source_target_pairs={{0,32},{32,0},{1,33},{33,1},{2,34},{34,2},{3,35},{35,3},{4,36},{36... | collective-permute-start | bytes 1572872 | tf_op jit(solution)/shard_map/ppermute | solution.py:212

commit v4 on v3

v4 whole, which is shorter than its diff:
```python
import jax
import jax.numpy as jnp
from jax import lax
from jax.experimental import pallas as pl
from jax.experimental.pallas import tpu as pltpu
from jax.sharding import Mesh, PartitionSpec as P


CLASSES = 3
FINE = 16
LIMIT = 32 << 20
F32 = jnp.float32
BF16 = jnp.bfloat16
VMEM = pl.BlockSpec(memory_space=pltpu.VMEM)


def prepare_body(energy, amps_ref, freqs_ref, class_ref, own_ref, square_ref, kind_ref):
    amps = amps_ref[...].astype(F32).T.astype(BF16)
    freqs = freqs_ref[...].astype(F32).T.astype(BF16)
    for k in range(own_ref.shape[0]):
        own_ref[k, 0] = amps
        own_ref[k, 1] = freqs
    for c in range(CLASSES):
        square_ref[c] = jnp.full(square_ref.shape[1:], energy[c] * energy[c], F32)
    kind_ref[...] = class_ref[...]


def prepare(screened, poles, gap_energy, gap_class, copies):
    rows, columns = screened.shape
    return pl.pallas_call(
        prepare_body,
        out_shape=(
            jax.ShapeDtypeStruct((copies, 2, columns, rows), BF16),
            jax.ShapeDtypeStruct((CLASSES, 8, rows), F32),
            jax.ShapeDtypeStruct(gap_class.shape, jnp.int32),
        ),
        grid=(1,),
        in_specs=[
            pl.BlockSpec(memory_space=pltpu.SMEM),
            pl.BlockSpec(screened.shape, lambda t: (0, 0)),
            pl.BlockSpec(poles.shape, lambda t: (0, 0)),
            pl.BlockSpec(gap_class.shape, lambda t: (0, 0)),
        ],
        out_specs=(VMEM, VMEM, VMEM),
        compiler_params=pltpu.CompilerParams(vmem_limit_bytes=8 << 20),
        name="prepare",
    )(*(pltpu.with_memory_space_constraint(a, pltpu.HBM) for a in (gap_energy, screened, poles, gap_class)))


def factors(group, start, blocks, square_ref):
    squares = [square_ref[c, 0:1, :] for c in range(CLASSES)]
    columns = [[] for _ in range(CLASSES)]
    for j in range(blocks):
        amps = group[start + j, 0].astype(F32)
        freqs = group[start + j, 1].astype(F32)
        square = freqs * freqs
        d0, d1, d2 = (square + e for e in squares)
        d12 = d1 * d2
        ratio = amps * freqs / (d0 * d12)
        r0 = ratio * d0
        columns[0].append((ratio * d12).astype(BF16))
        columns[1].append((r0 * d2).astype(BF16))
        columns[2].append((r0 * d1).astype(BF16))
    return jnp.concatenate([jnp.concatenate(c, axis=1) for c in columns], axis=0)


def first_body(place, square_ref, y_ref, inter_ref, split_ref, flat_ref, acc, near_ref, same_ref, cross_ref, right_ref, sems):
    step = pl.program_id(0)
    bands, blocks, size, states = inter_ref.shape
    own_z, core = place[0], place[1]
    half = size // 2
    copies = [
        pltpu.make_async_copy(split_ref.at[:, own_z, :, 1 - core], near_ref, sems.at[0]),
        pltpu.make_async_copy(split_ref.at[:, 1 - own_z, :, core], same_ref, sems.at[1]),
        pltpu.make_async_copy(split_ref.at[:, 1 - own_z, :, 1 - core], cross_ref, sems.at[2]),
        pltpu.make_async_copy(flat_ref.at[:, place[2]], right_ref.at[:, :size], sems.at[3]),
        pltpu.make_async_copy(flat_ref.at[:, place[3], half:], right_ref.at[:, size:], sems.at[4]),
    ]

    @pl.when(step == 0)
    def _():
        for copy in copies:
            copy.start()
        acc[...] = jnp.zeros_like(acc)

    factor = factors(y_ref, step * blocks, blocks, square_ref)
    for b in range(bands):
        rows = inter_ref[b].reshape(blocks * size, states)
        acc[b] += jnp.dot(factor, rows, preferred_element_type=F32)

    @pl.when(step == pl.num_programs(0) - 1)
    def _():
        for copy in copies:
            copy.wait()


def second_body(square_ref, cy_ref, zd_ref, zo_ref, near_ref, same_ref, acc_in, acc, far):
    bands, blocks, size, states = near_ref.shape
    factor = factors(cy_ref, 0, blocks, square_ref)
    cross = jnp.concatenate([factors(zd_ref, 0, blocks, square_ref), factors(zo_ref, 0, blocks, square_ref)], axis=0)
    for b in range(bands):
        rows = near_ref[b].reshape(blocks * size, states)
        acc[b] = acc_in[b] + jnp.dot(factor, rows, preferred_element_type=F32)
        rows = same_ref[b].reshape(blocks * size, states)
        far[b] = jnp.dot(cross, rows, preferred_element_type=F32)


def chosen(kind, terms):
    side = jnp.zeros_like(terms[0])
    for c in range(CLASSES):
        side = jnp.where(kind == c, terms[c], side)
    return side.astype(BF16)


def third_body(square_ref, kind_ref, czd_ref, czo_ref, cross_ref, right_ref, acc, far_in, keep_ref, send_ref, full):
    bands, blocks, size, states = cross_ref.shape
    half = size // 2
    cross = jnp.concatenate([factors(czd_ref, 0, blocks, square_ref), factors(czo_ref, 0, blocks, square_ref)], axis=0)
    sides = []
    for b in range(bands):
        rows = cross_ref[b].reshape(blocks * size, states)
        far = far_in[b] + jnp.dot(cross, rows, preferred_element_type=F32)
        kind = kind_ref[b : b + 1, :]
        low = [acc[b, c * size : c * size + half, :] + far[c * half : (c + 1) * half, :] for c in range(CLASSES)]
        high = [acc[b, c * size + half : (c + 1) * size, :] for c in range(CLASSES)]
        away = [far[(CLASSES + c) * half : (CLASSES + c + 1) * half, :] for c in range(CLASSES)]
        sides += [chosen(kind, low), chosen(kind, high), chosen(kind, away)]
    left = jnp.concatenate(sides, axis=0)
    right = right_ref[...].reshape(bands * (size + half), states)
    total = lax.dot_general(left, right, (((0,), (0,)), ((), ())), preferred_element_type=F32)
    full[...] = total.reshape(full.shape)
    core = lax.axis_index("c")
    keep_ref[...] = full[:, core]
    send_ref[...] = full[:, 1 - core]


def work(acc, blocks, size, steps):
    flops = 2 * acc.shape[0] * acc.shape[1] * acc.shape[2] * blocks * size * steps
    return pl.CostEstimate(flops=flops, bytes_accessed=1 << 20, transcendentals=0)


def first(place, square, y_group, intersections):
    bands, rows, states = intersections.shape
    per, size = y_group.shape[0], y_group.shape[3]
    blocks = per // 2
    split = pltpu.with_memory_space_constraint(intersections.reshape(bands, 2, per, 2, size, states), pltpu.HBM)
    flat = pltpu.with_memory_space_constraint(intersections.reshape(bands, rows // size, size, states), pltpu.HBM)
    acc = jax.ShapeDtypeStruct((bands, CLASSES * size, states), F32)
    part = jax.ShapeDtypeStruct((bands, per, size, states), BF16)
    right = jax.ShapeDtypeStruct((bands, size + size // 2, states), BF16)
    return pl.pallas_call(
        first_body,
        out_shape=(acc, part, part, part, right),
        grid_spec=pltpu.PrefetchScalarGridSpec(
            num_scalar_prefetch=1,
            grid=(2,),
            in_specs=[
                VMEM,
                VMEM,
                pl.BlockSpec((bands, None, blocks, None, size, states), lambda t, place: (0, place[0], t, place[1], 0, 0)),
                pl.BlockSpec(memory_space=pltpu.HBM),
                pl.BlockSpec(memory_space=pltpu.HBM),
            ],
            out_specs=(VMEM,) * 5,
            scratch_shapes=[pltpu.SemaphoreType.DMA((5,))],
        ),
        compiler_params=pltpu.CompilerParams(dimension_semantics=("arbitrary",), vmem_limit_bytes=LIMIT),
        cost_estimate=work(acc, blocks, size, 2),
        name="first",
    )(place, square, y_group, split, split, flat)


def second(square, cy_group, zd_group, zo_group, near, same, acc):
    shape = jax.ShapeDtypeStruct(acc.shape, F32)
    return pl.pallas_call(
        second_body,
        out_shape=(shape, shape),
        in_specs=[VMEM] * 7,
        out_specs=(VMEM, VMEM),
        compiler_params=pltpu.CompilerParams(vmem_limit_bytes=LIMIT),
        cost_estimate=work(acc, *near.shape[1:3], 2),
        name="second",
    )(square, cy_group, zd_group, zo_group, near, same, acc)


def third(square, kind, czd_group, czo_group, cross, right, acc, far):
    outer, states = acc.shape[2] // (2 * FINE), acc.shape[2]
    half = jax.ShapeDtypeStruct((outer, FINE, states), F32)
    return pl.pallas_call(
        third_body,
        out_shape=(half, half),
        in_specs=[VMEM] * 8,
        out_specs=(VMEM, VMEM),
        scratch_shapes=[pltpu.VMEM((outer, 2, FINE, states), F32)],
        compiler_params=pltpu.CompilerParams(vmem_limit_bytes=LIMIT),
        cost_estimate=work(acc, *cross.shape[1:3], 1),
        name="third",
    )(square, kind, czd_group, czo_group, cross, right, acc, far)


def local(intersections, screened, poles, gap_energy, gap_class):
    zl, c = lax.axis_index("zl"), lax.axis_index("c")
    zh, x = lax.axis_index("zh"), lax.axis_index("x")
    along = lax.axis_size("zh")
    beside = lax.rem(zh + jnp.where(zl == 0, along - 1, 1), along)
    place = jnp.stack([zl, c, zh * lax.axis_size("x") + x, beside * lax.axis_size("x") + x]).astype(jnp.int32)
    swap = [(0, 1), (1, 0)]
    aside = [(k, along + (k - 1) % along) for k in range(along)] + [(along + k, (k + 1) % along) for k in range(along)]
    per = lax.axis_size("y")
    own, square, kind = prepare(screened, poles, gap_energy, gap_class, per)
    y_group = lax.all_to_all(own, "y", 0, 0, tiled=True)
    half = y_group.shape[2] // 2
    zd_group = lax.ppermute(y_group[:, :, :half], "zl", swap)
    zo_group = lax.ppermute(y_group[:, :, half:], ("zl", "zh"), aside)
    cy_group = lax.ppermute(y_group, "c", swap)
    acc, near, same, cross, right = first(place, square, y_group, intersections)
    czd_group = lax.ppermute(zd_group, "c", swap)
    czo_group = lax.ppermute(zo_group, "c", swap)
    acc, far = second(square, cy_group, zd_group, zo_group, near, same, acc)
    keep, send = third(square, kind, czd_group, czo_group, cross, right, acc, far)
    chip = keep + lax.ppermute(send, "c", swap)
    pieces = lax.all_to_all(chip.astype(BF16), ("zl", "y"), 0, 0, tiled=True)
    rows = jnp.sum(pieces.astype(F32), axis=0)
    columns = lax.axis_size("zh") * lax.axis_size("x")
    fine = rows.shape[0]
    split = rows.reshape(fine, columns, -1).transpose(1, 0, 2)
    wide = split.shape[2]
    blocks = lax.all_to_all(split.reshape(columns, fine * wide), ("zh", "x"), 0, 0, tiled=True)
    total = jnp.sum(blocks, axis=0).reshape(fine, wide)
    count = intersections.shape[1] * intersections.shape[0] * 2 * per * 2
    return total * (1.0 / jnp.sqrt(F32(count)))


def solution(mesh):
    fine = Mesh(mesh.devices.reshape(2, 8, 2, 4, 8), ("zl", "y", "c", "zh", "x"))
    band, col = ("zl", "y", "c"), ("zh", "x")
    return jax.shard_map(
        local,
        mesh=fine,
        in_specs=(P(band, None, None), P(band, col), P(band, col), P(), P(band, None)),
        out_specs=P(band, col),
        check_vma=False,
    )
```

time: 105 us -> 105 us (level)
  starting transfers between devices: 8.18 us -> 24.4 us
  blocking collectives: 76.3 us -> 63.5 us
  waiting for transfers between devices: 8.96 us -> 6.32 us
    ppermute x2 -> x4, starting transfers between devices: 3.82 us -> 20.1 us  [the longest x1 14.1 us: local(): zo_group = lax.ppermute(y_group[:, :, half:], ('zl', 'zh'), aside)]
    all_to_all x1, blocking collectives: 32.4 us -> 21.5 us  [local(): lax.all_to_all(split.reshape(columns, fine * wide), ('zh', 'x'), 0, 0, ti...]
    ppermute x2 -> x4, waiting for transfers between devices: 7.44 us -> 4.8 us  [the longest x1 4.79 us: local(): zo_group = lax.ppermute(y_group[:, :, half:], ('zl', 'zh'), aside)]
    all_to_all x1, blocking collectives: 16.7 us -> 14.8 us  [local(): pieces = lax.all_to_all(chip.astype(BF16), ('zl', 'y'), 0, 0, tiled=True)]
  transfers between devices with their start and end apart: 4 -> 6, of which waited for: 2 -> 2; matrix products, arithmetic and copies ran while one was open for 0% -> 0% of each run, Pallas kernels for 7% -> 6%
where the time goes in v4:
time: 105 us
  blocking collectives  63.5 us (60%)
  starting transfers between devices  24.4 us (23%)
  Pallas kernels  9.12 us (9%)
  waiting for transfers between devices  6.32 us (6%)
    all_to_all x1, blocking collectives, local(): y_group = lax.all_to_all(own, 'y', 0, 0, tiled=True)  27.2 us
    all_to_all x1, blocking collectives, local(): lax.all_to_all(split.reshape(columns, fine * wide), ('zh', 'x'), 0, 0, ti...  21.5 us
    all_to_all x1, blocking collectives, local(): pieces = lax.all_to_all(chip.astype(BF16), ('zl', 'y'), 0, 0, tiled=True)  14.8 us
    ppermute x1, starting transfers between devices, local(): zo_group = lax.ppermute(y_group[:, :, half:], ('zl', 'zh'), aside)  14.1 us
    ppermute x1, waiting for transfers between devices, local(): zo_group = lax.ppermute(y_group[:, :, half:], ('zl', 'zh'), aside)  4.79 us
    pallas_call x1, Pallas kernels, first(): pl.pallas_call(first_body, out_shape=(acc, part, part, part, right), grid...  4.76 us
    ppermute x1, starting transfers between devices, local(): chip = keep + lax.ppermute(send, 'c', swap)  2.43 us
    ppermute x1, starting transfers between devices, local(): czd_group = lax.ppermute(zd_group, 'c', swap)  2.13 us
  transfers between devices with their start and end apart: 6, of which 2 were waited for; matrix products, arithmetic and copies ran while one was open for 0% of the time, Pallas kernels for 6%

profile of v4, /device:TPU:16, one launch (start us, length us, event | category | flops | bytes accessed | tf_op | source)
XLA Modules:
  0.0 104.8 jit_solution(6742778635048111848)
XLA Ops:
  0.0 0.9 prepare.1
  0.9 27.2 %all_to_all.19.y_ref = bf16[8,2,128,128]{3,2,1,0:T(8,128)(2,1)S(1)} all-to-all(bf16[8,2,128,128]{3,2,1,0:T(8,128)(2,1)S(1)} %get-tuple-element.19), channel_id=1, replica_groups=mesh['zl'=2,'y'=8,'c'=2,'zh'=4,'x'=8] {'y'}, dimensions={0} | all-to-all | bytes 1048576 | tf_op jit(solution)/shard_map/all_to_all | solution.py:211
  28.1 1.9 %collective-permute-start.4 = (bf16[8,2,128,128]{3,2,1,0:T(8,128)(2,1)S(1)}, bf16[8,2,128,128]{3,2,1,0:T(8,128)(2,1)S(1)}, u32[]{:S(2)}, u32[]{:S(2)}) collective-permute-start(bf16[8,2,128,128]{3,2,1,0:T(8,128)(2,1)S(1)} %all_to_all.19.y_ref), channel_id=1, source_target_pairs={{0,32},{32,0},{1,33},{33,1},{2,34},{34,2},{3,35},{35,3},{4,36},{36... | collective-permute-start | bytes 1572872 | tf_op jit(solution)/shard_map/ppermute | solution.py:215
  30.1 1.9 %collective-permute-start = (bf16[8,2,64,128]{3,2,1,0:T(8,128)(2,1)S(1)}, bf16[8,2,64,128]{3,2,1,0:T(8,128)(2,1)S(1)}, u32[]{:S(2)}, u32[]{:S(2)}) collective-permute-start(bf16[8,2,64,128]{3,2,1,0:T(8,128)(2,1)S(1)} %get-tuple-element.30), channel_id=1, source_target_pairs={{0,512},{512,0},{1,513},{513,1},{2,514},{514,2},{3,515},{515,3},{4... | collective-permute-start | bytes 786440 | tf_op jit(solution)/shard_map/ppermute | solution.py:213
  32.0 14.1 %collective-permute-start.2 = (bf16[8,2,64,128]{3,2,1,0:T(8,128)(2,1)S(1)}, bf16[8,2,64,128]{3,2,1,0:T(8,128)(2,1)S(1)}, u32[]{:S(2)}, u32[]{:S(2)}) collective-permute-start(bf16[8,2,64,128]{3,2,1,0:T(8,128)(2,1)S(1)} %get-tuple-element.29), channel_id=1, source_target_pairs={{0,536},{8,512},{16,520},{24,528},{512,8},{520,16},{528,24},{536,0... | collective-permute-start | bytes 786440 | tf_op jit(solution)/shard_map/ppermute | solution.py:214
  46.2 2.1 %collective-permute-start.1 = (bf16[8,2,64,128]{3,2,1,0:T(8,128)(2,1)S(1)}, bf16[8,2,64,128]{3,2,1,0:T(8,128)(2,1)S(1)}, u32[]{:S(2)}, u32[]{:S(2)}) collective-permute-start(bf16[8,2,64,128]{3,2,1,0:T(8,128)(2,1)S(1)} %collective-permute-done.zd_ref), channel_id=1, source_target_pairs={{0,32},{32,0},{1,33},{33,1},{2,34},{34,2},{3,35},{35,3},{4,36},{36... | collective-permute-start | bytes 786440 | tf_op jit(solution)/shard_map/ppermute | solution.py:217
  48.3 4.8 %collective-permute-done.2.zo_ref = bf16[8,2,64,128]{3,2,1,0:T(8,128)(2,1)S(1)} collective-permute-done((bf16[8,2,64,128]{3,2,1,0:T(8,128)(2,1)S(1)}, bf16[8,2,64,128]{3,2,1,0:T(8,128)(2,1)S(1)}, u32[]{:S(2)}, u32[]{:S(2)}) %collective-permute-start.2) | collective-permute-done | bytes 262176 | tf_op jit(solution)/shard_map/ppermute | solution.py:214
  53.1 1.9 %collective-permute-start.3 = (bf16[8,2,64,128]{3,2,1,0:T(8,128)(2,1)S(1)}, bf16[8,2,64,128]{3,2,1,0:T(8,128)(2,1)S(1)}, u32[]{:S(2)}, u32[]{:S(2)}) collective-permute-start(bf16[8,2,64,128]{3,2,1,0:T(8,128)(2,1)S(1)} %collective-permute-done.2.zo_ref), channel_id=1, source_target_pairs={{0,32},{32,0},{1,33},{33,1},{2,34},{34,2},{3,35},{35,3},{4,36},{36... | collective-permute-start | bytes 786440 | tf_op jit(solution)/shard_map/ppermute | solution.py:218
  55.0 0.1 pad_add_fusion.place
  55.1 4.8 %first.1 = (f32[2,384,512]{2,1,0:T(8,128)S(1)}, bf16[2,8,128,512]{3,2,1,0:T(8,128)(2,1)S(1)}, bf16[2,8,128,512]{3,2,1,0:T(8,128)(2,1)S(1)}, bf16[2,8,128,512]{3,2,1,0:T(8,128)(2,1)S(1)}, bf16[2,192,512]{2,1,0:T(8,128)(2,1)S(1)}) custom-call(s32[4]{0:T(128)S(1)} %pad_add_fusion.place, f32[3,8,128]{2,1,0:T(8,128)S(1)} %get-tuple-element.17.square_ref, ...), custom_call_target="tpu_custom_call" | custom-call | flops 805306368 | bytes 1048576 | tf_op jit(solution)/shard_map/first/pallas_call | solution.py:151
  59.9 1.9 %second.1 = (f32[2,384,512]{2,1,0:T(8,128)S(1)}, f32[2,384,512]{2,1,0:T(8,128)S(1)}) custom-call(f32[3,8,128]{2,1,0:T(8,128)S(1)} %get-tuple-element.17.square_ref, bf16[8,2,128,128]{3,2,1,0:T(8,128)(2,1)S(1)} %collective-permute-done.4.cy_ref, bf16[8,2,64,128]{3,2,1,0:T(8,128)(2,1)S(1)} %collective-permute-done.zd_ref, ...), custom_call_target="tpu_custom_call" | custom-call | flops 1610612736 | bytes 1048576 | tf_op jit(solution)/shard_map/second/pallas_call | solution.py:175
  61.7 0.0 collective-permute-done.1.czd_ref
  61.8 0.0 collective-permute-done.3.czo_ref
  61.8 1.6 %third.1 = (f32[16,16,512]{2,1,0:T(8,128)S(1)}, f32[16,16,512]{2,1,0:T(8,128)S(1)}) custom-call(f32[3,8,128]{2,1,0:T(8,128)S(1)} %get-tuple-element.17.square_ref, s32[2,512]{1,0:T(2,128)S(1)} %get-tuple-element.18.kind_ref, bf16[8,2,64,128]{3,2,1,0:T(8,128)(2,1)S(1)} %collective-permute-done.1.czd_ref, ...), custom_call_target="tpu_custom_call" | custom-call | flops 805306368 | bytes 1048576 | tf_op jit(solution)/shard_map/third/pallas_call | solution.py:189
  63.4 2.4 %collective-permute-start.5 = (f32[16,16,512]{2,1,0:T(8,128)S(1)}, f32[16,16,512]{2,1,0:T(8,128)S(1)}, u32[]{:S(2)}, u32[]{:S(2)}) collective-permute-start(f32[16,16,512]{2,1,0:T(8,128)S(1)} %get-tuple-element.28), channel_id=1, source_target_pairs={{0,32},{32,0},{1,33},{33,1},{2,34},{34,2},{3,35},{35,3},{4,36},{36... | collective-permute-start | bytes 1572872 | tf_op jit(solution)/shard_map/ppermute | solution.py:221
  65.8 1.5 %collective-permute-done.5 = f32[16,16,512]{2,1,0:T(8,128)S(1)} collective-permute-done((f32[16,16,512]{2,1,0:T(8,128)S(1)}, f32[16,16,512]{2,1,0:T(8,128)S(1)}, u32[]{:S(2)}, u32[]{:S(2)}) %collective-permute-start.5) | collective-permute-done | bytes 524320 | tf_op jit(solution)/shard_map/ppermute | solution.py:221
  67.3 0.1 add_convert_fusion
  67.4 14.8 %all_to_all.20 = bf16[16,16,512]{2,1,0:T(8,128)(2,1)S(1)} all-to-all(bf16[16,16,512]{2,1,0:T(8,128)(2,1)S(1)} %add_convert_fusion), channel_id=1, replica_groups=mesh['zl'=2,'y'=8,'c'=2,'zh'=4,'x'=8] {'zl','y'}, dimensions={0} | all-to-all | bytes 524288 | tf_op jit(solution)/shard_map/all_to_all | solution.py:222
  82.2 0.1 reshape.18
  82.4 0.1 copy.7
  82.5 0.1 copy.8
  82.6 21.5 %all_to_all.21 = f32[32,1,256]{2,1,0:T(1,128)S(1)} all-to-all(f32[32,1,256]{2,1,0:T(1,128)S(1)} %copy.8), channel_id=1, replica_groups=mesh['zl'=2,'y'=8,'c'=2,'zh'=4,'x'=8] {'zh','x'}, dimensions={0} | all-to-all | bytes 65536 | tf_op jit(solution)/shard_map/all_to_all | solution.py:228
  104.0 0.1 reduce_sum.19
  104.1 0.7 mul.19
  (5 shorter events, 0.1 us)
Async XLA Ops:
  28.1 31.7 %collective-permute-start.4 = (bf16[8,2,128,128]{3,2,1,0:T(8,128)(2,1)S(1)}, bf16[8,2,128,128]{3,2,1,0:T(8,128)(2,1)S(1)}, u32[]{:S(2)}, u32[]{:S(2)}) collective-permute-start(bf16[8,2,128,128]{3,2,1,0:T(8,128)(2,1)S(1)} %all_to_all.19.y_ref), channel_id=1, source_target_pairs={{0,32},{32,0},{1,33},{33,1},{2,34},{34,2},{3,35},{35,3},{4,36},{36... | collective-permute-start | bytes 1572872 | tf_op jit(solution)/shard_map/ppermute | solution.py:215
  30.1 16.1 %collective-permute-start = (bf16[8,2,64,128]{3,2,1,0:T(8,128)(2,1)S(1)}, bf16[8,2,64,128]{3,2,1,0:T(8,128)(2,1)S(1)}, u32[]{:S(2)}, u32[]{:S(2)}) collective-permute-start(bf16[8,2,64,128]{3,2,1,0:T(8,128)(2,1)S(1)} %get-tuple-element.30), channel_id=1, source_target_pairs={{0,512},{512,0},{1,513},{513,1},{2,514},{514,2},{3,515},{515,3},{4... | collective-permute-start | bytes 786440 | tf_op jit(solution)/shard_map/ppermute | solution.py:213
  32.0 21.1 %collective-permute-start.2 = (bf16[8,2,64,128]{3,2,1,0:T(8,128)(2,1)S(1)}, bf16[8,2,64,128]{3,2,1,0:T(8,128)(2,1)S(1)}, u32[]{:S(2)}, u32[]{:S(2)}) collective-permute-start(bf16[8,2,64,128]{3,2,1,0:T(8,128)(2,1)S(1)} %get-tuple-element.29), channel_id=1, source_target_pairs={{0,536},{8,512},{16,520},{24,528},{512,8},{520,16},{528,24},{536,0... | collective-permute-start | bytes 786440 | tf_op jit(solution)/shard_map/ppermute | solution.py:214
  46.2 15.6 %collective-permute-start.1 = (bf16[8,2,64,128]{3,2,1,0:T(8,128)(2,1)S(1)}, bf16[8,2,64,128]{3,2,1,0:T(8,128)(2,1)S(1)}, u32[]{:S(2)}, u32[]{:S(2)}) collective-permute-start(bf16[8,2,64,128]{3,2,1,0:T(8,128)(2,1)S(1)} %collective-permute-done.zd_ref), channel_id=1, source_target_pairs={{0,32},{32,0},{1,33},{33,1},{2,34},{34,2},{3,35},{35,3},{4,36},{36... | collective-permute-start | bytes 786440 | tf_op jit(solution)/shard_map/ppermute | solution.py:217
  53.1 8.7 %collective-permute-start.3 = (bf16[8,2,64,128]{3,2,1,0:T(8,128)(2,1)S(1)}, bf16[8,2,64,128]{3,2,1,0:T(8,128)(2,1)S(1)}, u32[]{:S(2)}, u32[]{:S(2)}) collective-permute-start(bf16[8,2,64,128]{3,2,1,0:T(8,128)(2,1)S(1)} %collective-permute-done.2.zo_ref), channel_id=1, source_target_pairs={{0,32},{32,0},{1,33},{33,1},{2,34},{34,2},{3,35},{35,3},{4,36},{36... | collective-permute-start | bytes 786440 | tf_op jit(solution)/shard_map/ppermute | solution.py:218
  63.4 4.0 %collective-permute-start.5 = (f32[16,16,512]{2,1,0:T(8,128)S(1)}, f32[16,16,512]{2,1,0:T(8,128)S(1)}, u32[]{:S(2)}, u32[]{:S(2)}) collective-permute-start(f32[16,16,512]{2,1,0:T(8,128)S(1)} %get-tuple-element.28), channel_id=1, source_target_pairs={{0,32},{32,0},{1,33},{33,1},{2,34},{34,2},{3,35},{35,3},{4,36},{36... | collective-permute-start | bytes 1572872 | tf_op jit(solution)/shard_map/ppermute | solution.py:221

commit v5 on v3

--- a/solution.py
+++ b/solution.py
@@ -106,7 +106,7 @@
         acc[b] = acc_in[b] + jnp.dot(factor, rows, preferred_element_type=F32)
 
 
-def third_body(square_ref, kind_ref, cz_ref, inter_ref, right_ref, acc_in, keep_ref, send_ref, full):
+def third_body(square_ref, kind_ref, cz_ref, inter_ref, right_ref, acc_in, full_ref):
     bands, blocks, size, states = inter_ref.shape
     factor = factors(cz_ref, 0, blocks, square_ref)
     sides = []
@@ -121,10 +121,9 @@
     left = jnp.concatenate(sides, axis=0)
     right = right_ref[...].reshape(bands * size, states)
     total = lax.dot_general(left, right, (((0,), (0,)), ((), ())), preferred_element_type=F32)
-    full[...] = total.reshape(full.shape)
-    core = lax.axis_index("c")
-    keep_ref[...] = full[:, core]
-    send_ref[...] = full[:, 1 - core]
+    total = total.reshape(full_ref.shape[1], 2, FINE, states)
+    full_ref[0] = total[:, 0]
+    full_ref[1] = total[:, 1]
 
 
 def work(acc, blocks, size, steps):
@@ -182,13 +181,11 @@
 
 def third(square, kind, cz_group, inter, right, acc):
     outer, states = acc.shape[2] // (2 * FINE), acc.shape[2]
-    half = jax.ShapeDtypeStruct((outer, FINE, states), F32)
     return pl.pallas_call(
         third_body,
-        out_shape=(half, half),
+        out_shape=jax.ShapeDtypeStruct((2, outer, FINE, states), F32),
         in_specs=[VMEM] * 6,
-        out_specs=(VMEM, VMEM),
-        scratch_shapes=[pltpu.VMEM((outer, 2, FINE, states), F32)],
+        out_specs=VMEM,
         compiler_params=pltpu.CompilerParams(vmem_limit_bytes=LIMIT),
         cost_estimate=work(acc, *inter.shape[1:3], 1),
         name="third",
@@ -208,15 +205,16 @@
     acc, same, cross, right = first(place, square, y_group, cy_group, intersections)
     cz_group = lax.ppermute(z_group, "c", swap)
     acc = second(square, z_group, same, acc)
-    keep, send = third(square, kind, cz_group, cross, right, acc)
-    chip = keep + lax.ppermute(send, "c", swap)
+    full = third(square, kind, cz_group, cross, right, acc)
+    pair = lax.all_to_all(full, "c", 0, 0, tiled=True)
+    chip = pair[0] + pair[1]
     pieces = lax.all_to_all(chip.astype(BF16), ("zl", "y"), 0, 0, tiled=True)
     rows = jnp.sum(pieces.astype(F32), axis=0)
-    columns = lax.axis_size("zh") * lax.axis_size("x")
+    high, low = lax.axis_size("zh"), lax.axis_size("x")
     fine = rows.shape[0]
-    split = rows.reshape(fine, columns, -1).transpose(1, 0, 2)
-    wide = split.shape[2]
-    blocks = lax.all_to_all(split.reshape(columns, fine * wide), ("zh", "x"), 0, 0, tiled=True)
+    split = rows.reshape(fine, high, low, -1).transpose(2, 1, 0, 3)
+    wide = split.shape[3]
+    blocks = lax.all_to_all(split.reshape(high * low, fine * wide), ("x", "zh"), 0, 0, tiled=True)
     total = jnp.sum(blocks, axis=0).reshape(fine, wide)
     count = intersections.shape[1] * intersections.shape[0] * 2 * per * 2
     return total * (1.0 / jnp.sqrt(F32(count)))

time: 105 us -> 105 us (level)
  blocking collectives: 76.3 us -> 80.5 us
  starting transfers between devices: 8.18 us -> 5.74 us
  waiting for transfers between devices: 8.96 us -> 7.44 us
    all_to_all x1 -> x2, blocking collectives: 32.4 us -> 36.9 us  [the longest x1 32.4 us: local(): lax.all_to_all(split.reshape(high * low, fine * wide), ('x', 'zh'), 0, 0,...]
    ppermute x1 -> x0, starting transfers between devices: 2.44 us -> none  [local(): chip = keep + lax.ppermute(send, 'c', swap)]
    ppermute x1 -> x0, waiting for transfers between devices: 1.51 us -> none  [local(): chip = keep + lax.ppermute(send, 'c', swap)]
  transfers between devices with their start and end apart: 4 -> 3, of which waited for: 2 -> 1; matrix products, arithmetic and copies ran while one was open for 0% -> 0% of each run, Pallas kernels for 7% -> 7%
where the time goes in v5:
time: 105 us
  blocking collectives  80.5 us (77%)
  Pallas kernels  9.47 us (9%)
  waiting for transfers between devices  7.44 us (7%)
  starting transfers between devices  5.74 us (5%)
  local copies, waits for them, and re-layouts  1.11 us (1%)
    all_to_all x1, blocking collectives, local(): lax.all_to_all(split.reshape(high * low, fine * wide), ('x', 'zh'), 0, 0,...  32.4 us
    all_to_all x1, blocking collectives, local(): y_group = lax.all_to_all(own, 'y', 0, 0, tiled=True)  27.2 us
    all_to_all x1, blocking collectives, local(): pieces = lax.all_to_all(chip.astype(BF16), ('zl', 'y'), 0, 0, tiled=True)  16.3 us
    ppermute x1, waiting for transfers between devices, local(): z_group = lax.ppermute(y_group, 'zl', swap)  7.44 us
    pallas_call x1, Pallas kernels, first(): pl.pallas_call(first_body, out_shape=(acc, half, half, right), grid_spec=...  6.24 us
    all_to_all x1, blocking collectives, local(): pair = lax.all_to_all(full, 'c', 0, 0, tiled=True)  4.58 us
  transfers between devices with their start and end apart: 3, of which 1 were waited for; matrix products, arithmetic and copies ran while one was open for 0% of the time, Pallas kernels for 7%

profile of v5, /device:TPU:16, one launch (start us, length us, event | category | flops | bytes accessed | tf_op | source)
XLA Modules:
  0.0 104.6 jit_solution(2943057467892671648)
XLA Ops:
  0.0 0.9 prepare.1
  0.9 27.2 %all_to_all.25.y_ref = bf16[8,2,128,128]{3,2,1,0:T(8,128)(2,1)S(1)} all-to-all(bf16[8,2,128,128]{3,2,1,0:T(8,128)(2,1)S(1)} %get-tuple-element.14), channel_id=1, replica_groups=mesh['zl'=2,'y'=8,'c'=2,'zh'=4,'x'=8] {'y'}, dimensions={0} | all-to-all | bytes 1048576 | tf_op jit(solution)/shard_map/all_to_all | solution.py:202
  28.1 1.9 %collective-permute-start = (bf16[8,2,128,128]{3,2,1,0:T(8,128)(2,1)S(1)}, bf16[8,2,128,128]{3,2,1,0:T(8,128)(2,1)S(1)}, u32[]{:S(2)}, u32[]{:S(2)}) collective-permute-start(bf16[8,2,128,128]{3,2,1,0:T(8,128)(2,1)S(1)} %all_to_all.25.y_ref), channel_id=1, source_target_pairs={{0,512},{512,0},{1,513},{513,1},{2,514},{514,2},{3,515},{515,3},{4... | collective-permute-start | bytes 1572872 | tf_op jit(solution)/shard_map/ppermute | solution.py:203
  30.0 1.9 %collective-permute-start.2 = (bf16[8,2,128,128]{3,2,1,0:T(8,128)(2,1)S(1)}, bf16[8,2,128,128]{3,2,1,0:T(8,128)(2,1)S(1)}, u32[]{:S(2)}, u32[]{:S(2)}) collective-permute-start(bf16[8,2,128,128]{3,2,1,0:T(8,128)(2,1)S(1)} %all_to_all.25.y_ref), channel_id=1, source_target_pairs={{0,32},{32,0},{1,33},{33,1},{2,34},{34,2},{3,35},{35,3},{4,36},{36... | collective-permute-start | bytes 1572872 | tf_op jit(solution)/shard_map/ppermute | solution.py:204
  32.0 7.4 %collective-permute-done.z_ref = bf16[8,2,128,128]{3,2,1,0:T(8,128)(2,1)S(1)} collective-permute-done((bf16[8,2,128,128]{3,2,1,0:T(8,128)(2,1)S(1)}, bf16[8,2,128,128]{3,2,1,0:T(8,128)(2,1)S(1)}, u32[]{:S(2)}, u32[]{:S(2)}) %collective-permute-start) | collective-permute-done | bytes 524320 | tf_op jit(solution)/shard_map/ppermute | solution.py:203
  39.4 1.9 %collective-permute-start.1 = (bf16[8,2,128,128]{3,2,1,0:T(8,128)(2,1)S(1)}, bf16[8,2,128,128]{3,2,1,0:T(8,128)(2,1)S(1)}, u32[]{:S(2)}, u32[]{:S(2)}) collective-permute-start(bf16[8,2,128,128]{3,2,1,0:T(8,128)(2,1)S(1)} %collective-permute-done.z_ref), channel_id=1, source_target_pairs={{0,32},{32,0},{1,33},{33,1},{2,34},{34,2},{3,35},{35,3},{4,36},{36... | collective-permute-start | bytes 1572872 | tf_op jit(solution)/shard_map/ppermute | solution.py:206
  41.3 0.1 pad_add_fusion.place
  41.4 0.0 collective-permute-done.2.cy_ref
  41.4 6.2 %first.1 = (f32[2,384,512]{2,1,0:T(8,128)S(1)}, bf16[2,8,128,512]{3,2,1,0:T(8,128)(2,1)S(1)}, bf16[2,8,128,512]{3,2,1,0:T(8,128)(2,1)S(1)}, bf16[2,128,512]{2,1,0:T(8,128)(2,1)S(1)}) custom-call(s32[3]{0:T(128)S(1)} %pad_add_fusion.place, f32[3,8,128]{2,1,0:T(8,128)S(1)} %get-tuple-element.12.square_ref, bf16[8,2,128,128]{3,2,1,0:T(8,128)(2,1)S(1)} %all_to_all.25.y_ref, ...), custom_call_target="tpu_custom_call" | custom-call | flops 1610612736 | bytes 1048576 | tf_op jit(solution)/shard_map/first/pallas_call | solution.py:147
  47.7 1.0 second.1.acc_in
  48.7 0.0 collective-permute-done.1.cz_ref
  48.7 1.3 %third.1 = f32[2,16,16,512]{3,2,1,0:T(8,128)S(1)} custom-call(f32[3,8,128]{2,1,0:T(8,128)S(1)} %get-tuple-element.12.square_ref, s32[2,512]{1,0:T(2,128)S(1)} %get-tuple-element.13.kind_ref, bf16[8,2,128,128]{3,2,1,0:T(8,128)(2,1)S(1)} %collective-permute-done.1.cz_ref, bf16[2,8,128,512]{3,2,1,0:T(8,128)(2,1)S(1)} %get-tuple-element.15.inter_ref, ...), custom_call_target="tpu_custom_call" | custom-call | flops 805306368 | bytes 1048576 | tf_op jit(solution)/shard_map/third/pallas_call | solution.py:184
  50.0 4.6 %all_to_all.26 = f32[2,16,16,512]{3,2,1,0:T(8,128)S(1)} all-to-all(f32[2,16,16,512]{3,2,1,0:T(8,128)S(1)} %third.1), channel_id=1, replica_groups=mesh['zl'=2,'y'=8,'c'=2,'zh'=4,'x'=8] {'c'}, dimensions={0} | all-to-all | bytes 2097152 | tf_op jit(solution)/shard_map/all_to_all | solution.py:209
  54.6 0.1 fusion.1
  54.6 16.3 %all_to_all.27 = bf16[16,16,512]{2,1,0:T(8,128)(2,1)S(1)} all-to-all(bf16[16,16,512]{2,1,0:T(8,128)(2,1)S(1)} %fusion.1), channel_id=1, replica_groups=mesh['zl'=2,'y'=8,'c'=2,'zh'=4,'x'=8] {'zl','y'}, dimensions={0} | all-to-all | bytes 524288 | tf_op jit(solution)/shard_map/all_to_all | solution.py:211
  71.0 0.1 reshape.20
  71.2 0.2 copy.7
  71.3 0.1 all_to_all.20
  71.5 32.4 %all_to_all.28 = f32[32,1,256]{2,1,0:T(1,128)S(1)} all-to-all(f32[32,1,256]{2,1,0:T(1,128)S(1)} %all_to_all.20), channel_id=1, replica_groups=mesh['zl'=2,'y'=8,'c'=2,'zh'=4,'x'=8] {'x','zh'}, dimensions={0} | all-to-all | bytes 65536 | tf_op jit(solution)/shard_map/all_to_all | solution.py:217
  103.8 0.1 reduce_sum.19
  103.9 0.7 mul.15
  (2 shorter events, 0.0 us)
Async XLA Ops:
  28.1 11.3 %collective-permute-start = (bf16[8,2,128,128]{3,2,1,0:T(8,128)(2,1)S(1)}, bf16[8,2,128,128]{3,2,1,0:T(8,128)(2,1)S(1)}, u32[]{:S(2)}, u32[]{:S(2)}) collective-permute-start(bf16[8,2,128,128]{3,2,1,0:T(8,128)(2,1)S(1)} %all_to_all.25.y_ref), channel_id=1, source_target_pairs={{0,512},{512,0},{1,513},{513,1},{2,514},{514,2},{3,515},{515,3},{4... | collective-permute-start | bytes 1572872 | tf_op jit(solution)/shard_map/ppermute | solution.py:203
  30.0 11.4 %collective-permute-start.2 = (bf16[8,2,128,128]{3,2,1,0:T(8,128)(2,1)S(1)}, bf16[8,2,128,128]{3,2,1,0:T(8,128)(2,1)S(1)}, u32[]{:S(2)}, u32[]{:S(2)}) collective-permute-start(bf16[8,2,128,128]{3,2,1,0:T(8,128)(2,1)S(1)} %all_to_all.25.y_ref), channel_id=1, source_target_pairs={{0,32},{32,0},{1,33},{33,1},{2,34},{34,2},{3,35},{35,3},{4,36},{36... | collective-permute-start | bytes 1572872 | tf_op jit(solution)/shard_map/ppermute | solution.py:204
  39.4 9.3 %collective-permute-start.1 = (bf16[8,2,128,128]{3,2,1,0:T(8,128)(2,1)S(1)}, bf16[8,2,128,128]{3,2,1,0:T(8,128)(2,1)S(1)}, u32[]{:S(2)}, u32[]{:S(2)}) collective-permute-start(bf16[8,2,128,128]{3,2,1,0:T(8,128)(2,1)S(1)} %collective-permute-done.z_ref), channel_id=1, source_target_pairs={{0,32},{32,0},{1,33},{33,1},{2,34},{34,2},{3,35},{35,3},{4,36},{36... | collective-permute-start | bytes 1572872 | tf_op jit(solution)/shard_map/ppermute | solution.py:206
